TPU v7x, 32 devices: a whole 2x2x4 slice. The times are simulated.
32 devices in a mesh: gx: 2 (over x), gy: 4 (over y, core), gz: 4 (over z).
Axes of the slice: x: 2, y: 2, z: 4, core: 2. Of those that a mesh axis runs over, the one named last changes fastest.
Arguments:
- panel: float32 [128, 131072], P(None, ('gx', 'gy', 'gz')), may hold values from -3000 to 3000
- trailing: float32 [64, 131072], P(None, ('gx', 'gy', 'gz')), may hold values from -6 to 6
Outputs:
- basis: float32 [128, 131072], P(None, ('gx', 'gy', 'gz'))
- upper: float32 [128, 128], replicated
- coupling: float32 [128, 64], replicated
- updated: float32 [64, 131072], P(None, ('gx', 'gy', 'gz'))
All inputs are finite; a program needn't handle non-finite values.
Results may differ from a plain program's by a relative error of at most 0.0033.
Values sent between devices are 32-bit elements; how exact they have to be, the bound alone decides.
A program may use at most 64 MiB of HBM per device.

v0:
```python
import functools

import jax
import jax.numpy as jnp
from jax import lax
from jax.experimental import pallas as pl
from jax.experimental.pallas import tpu as pltpu
from jax.sharding import PartitionSpec as P

MESH = pl.DeviceIdType.MESH
HIGHEST = lax.Precision.HIGHEST
NT = (((1,), (1,)), ((), ()))
NN = (((1,), (0,)), ((), ()))
VMEM = pl.BlockSpec(memory_space=pltpu.VMEM)
HBM = pl.BlockSpec(memory_space=pltpu.HBM)


def exact(left, right, dims):
    return lax.dot_general(left, right, dims, precision=HIGHEST, preferred_element_type=jnp.float32)


def terms(value, count):
    found = []
    for _ in range(count):
        term = value.astype(jnp.bfloat16)
        found.append(term)
        value = value - term.astype(jnp.float32)
    return found


def stacked(left, right, dims):
    return lax.dot_general(left, right, dims, preferred_element_type=jnp.float32)


def factor(tiles):
    size = tiles[0].shape[1]
    lane = lax.broadcasted_iota(jnp.int32, (1, size), 1)
    row_in_tile = lax.broadcasted_iota(jnp.int32, (8, 1), 0)
    lanes = lax.broadcasted_iota(jnp.int32, (8, size), 1)
    tiles = list(tiles)
    for at in range(len(tiles)):
        first = 8 * at
        inside = (lane >= first) & (lane < first + 8)
        columns = {h: [jnp.broadcast_to(tiles[h][:, first + j : first + j + 1], (8, size)) for j in range(8)] for h in range(at, len(tiles))}
        for h in range(at + 1, len(tiles)):
            tiles[h] = jnp.where(inside, 0.0, tiles[h])
        for r in range(8):
            k = first + r
            row = tiles[at][r : r + 1, :]
            unit = jnp.where(lane == k, 1.0, row)
            behind = jnp.where(inside & (lane > k), 0.0, unit)
            pivots = [columns[at][j][r : r + 1, :] for j in range(8)]
            over = 1.0 / pivots[r]
            for h in range(at, len(tiles)):
                if h == at and r == 7:
                    continue
                times = columns[h][r] * over
                for j in range(r + 1, 8):
                    columns[h][j] = columns[h][j] - times * pivots[j]
                if h == at:
                    below = row_in_tile > r
                    tiles[h] = jnp.where(below, jnp.where(lanes == k, 0.0, tiles[h]) - times * unit, tiles[h])
                else:
                    tiles[h] = tiles[h] - times * behind
    uppers, inverses = [], []
    for h, tile in enumerate(tiles):
        rows = row_in_tile + 8 * h
        pivot = jnp.sum(jnp.where(lanes == rows, tile, 0.0), axis=1, keepdims=True)
        root = jnp.sqrt(pivot)
        over = 1.0 / root
        uppers.append(jnp.where(lanes > rows, tile * over, jnp.where(lanes == rows, root, 0.0)))
        inverses.append(jnp.where(lanes < rows, tile * over, jnp.where(lanes == rows, over, 0.0)))
    return uppers, inverses


def greet(sizes):
    nx, ny, nz = sizes
    gx, gy, gz = lax.axis_index("gx"), lax.axis_index("gy"), lax.axis_index("gz")
    barrier = pltpu.get_barrier_semaphore()
    me = gx * ny + gy
    for step in range(1, nx * ny):
        peer = lax.rem(me + step, nx * ny)
        pl.semaphore_signal(barrier, inc=1, device_id=(peer // ny, lax.rem(peer, ny), gz), device_id_type=MESH)
    for step in range(1, nz):
        pl.semaphore_signal(barrier, inc=1, device_id=(gx, gy, lax.rem(gz + step, nz)), device_id_type=MESH)


def all_sum(sizes, send, landed, column, gathered, send_sem, recv_sem):
    nx, ny, nz = sizes
    group = nx * ny
    gx, gy, gz = lax.axis_index("gx"), lax.axis_index("gy"), lax.axis_index("gz")
    me = gx * ny + gy

    def plane_copy(src, dst, step, base):
        peer = lax.rem(me + step, group)
        return pltpu.make_async_remote_copy(
            src_ref=src(peer),
            dst_ref=dst,
            send_sem=send_sem.at[base + step],
            recv_sem=recv_sem.at[base + step],
            device_id=(peer // ny, lax.rem(peer, ny), gz),
            device_id_type=MESH,
        )

    out = [plane_copy(lambda peer: send.at[peer], landed.at[step], step, 0) for step in range(1, group)]
    for copy in out:
        copy.start()
    part = send[me]
    for step in range(1, group):
        out[step - 1].wait_recv()
        part = part + landed[step]
    column[gz] = part
    along = [
        pltpu.make_async_remote_copy(
            src_ref=column.at[gz],
            dst_ref=column.at[gz],
            send_sem=send_sem.at[group + step],
            recv_sem=recv_sem.at[group + step],
            device_id=(gx, gy, lax.rem(gz + step, nz)),
            device_id_type=MESH,
        )
        for step in range(1, nz)
    ]
    for copy in along:
        copy.start()
    for copy in along:
        copy.wait_recv()
    total = column[0]
    for z in range(1, nz):
        total = total + column[z]
    gathered[me] = total
    back = [plane_copy(lambda peer: gathered.at[me], gathered.at[me], step, group + nz) for step in range(1, group)]
    for copy in back:
        copy.start()
    for copy in back:
        copy.wait_recv()
    for copy in out + along + back:
        copy.wait_send()


def sum_scratch(sizes, rows, size):
    nx, ny, nz = sizes
    group = nx * ny
    return [
        pltpu.VMEM((group, rows, size), jnp.float32),
        pltpu.VMEM((group, rows, size), jnp.float32),
        pltpu.VMEM((nz, rows, size), jnp.float32),
        pltpu.SemaphoreType.DMA((2 * group + nz,)),
        pltpu.SemaphoreType.DMA((2 * group + nz,)),
    ]


def chunk_of(width, most):
    return most if width % most == 0 else width


def reduce_kernel(sizes, panel, trailing, first, upper, summed, panel_held, trailing_held, first_held, move_sem, upper_held, *scratch):
    size, width = panel.shape
    trail = trailing.shape[0]
    group = sizes[0] * sizes[1]
    rows, less = size // group, trail // group
    chunk = chunk_of(width, 1024)
    greet(sizes)
    loads, more, stores = [], [], []
    for i in range(width // chunk):
        at = pl.ds(i * chunk, chunk)
        loads.append(pltpu.make_async_copy(panel.at[:, at], panel_held.at[:, at], move_sem.at[0, i]))
        loads[-1].start()
    for i in range(width // chunk):
        at = pl.ds(i * chunk, chunk)
        more.append(pltpu.make_async_copy(trailing.at[:, at], trailing_held.at[:, at], move_sem.at[1, i]))
        more[-1].start()
    both = jnp.zeros((2 * size, 2 * size), jnp.float32)
    small = jnp.zeros((size, size), jnp.float32)
    for i in range(width // chunk):
        loads[i].wait()
        high, middle, low = terms(panel_held[:, i * chunk : (i + 1) * chunk], 3)
        pair = jnp.concatenate([high, middle], axis=0)
        both = both + stacked(pair, pair, NT)
        small = small + stacked(high, low, NT)
    small = small + both[:size, size:]
    gram = both[:size, :size] + ((small + small.T) + both[size:, size:])
    gathered, *first_sum = scratch[:6]
    for p in range(group):
        first_sum[0][p] = gram[p * rows : (p + 1) * rows]
    pl.semaphore_wait(pltpu.get_barrier_semaphore(), group - 1 + sizes[2] - 1)
    all_sum(sizes, first_sum[0], first_sum[1], first_sum[2], gathered, *first_sum[3:])
    gram = jnp.concatenate([gathered[p] for p in range(group)], axis=0)
    uppers, inverses = factor([gram[h : h + 8] for h in range(0, size, 8)])
    for h in range(len(uppers)):
        upper_held[8 * h : 8 * h + 8] = uppers[h]
    stores.append(pltpu.make_async_copy(upper_held, upper, move_sem.at[3, 0]))
    stores[-1].start()
    inverse = jnp.concatenate(inverses, axis=0)
    one, two, three = terms(inverse, 3)
    left = jnp.concatenate([three, one, two, two, one, one], axis=1)
    total = jnp.zeros((size + 2 * trail, 2 * size), jnp.float32)
    for i in range(width // chunk):
        at = pl.ds(i * chunk, chunk)
        high, middle, low = terms(panel_held[:, at], 3)
        basis = stacked(left, jnp.concatenate([high, low, middle, high, middle, high], axis=0), NN)
        first_held[:, at] = basis
        stores.append(pltpu.make_async_copy(first_held.at[:, at], first.at[:, at], move_sem.at[2, i]))
        stores[-1].start()
        high, low = terms(basis, 2)
        more[i].wait()
        c_high, c_low = terms(trailing_held[:, at], 2)
        left_terms = jnp.concatenate([high, c_high, c_low], axis=0)
        total = total + stacked(left_terms, jnp.concatenate([high, low], axis=0), NT)
    mixed = total[:size, size:]
    own = total[:size, :size] + (mixed + mixed.T)
    cross = total[size:, :size] + total[size:, size:]
    cross = cross[:trail] + cross[trail:]
    second_sum = scratch[6:]
    for p in range(group):
        second_sum[0][p, :rows] = own[p * rows : (p + 1) * rows]
        second_sum[0][p, rows:] = cross[p * less : (p + 1) * less]
    all_sum(sizes, second_sum[0], second_sum[1], second_sum[2], summed, *second_sum[3:])
    for store in stores:
        store.wait()


def final_kernel(scale, summed, upper_one, first, trailing, basis, upper, coupling, updated, first_held, trailing_held, basis_held, updated_held, one_held, upper_held, coupling_held, load_sem, store_sem):
    size, width = first.shape
    loads = [
        pltpu.make_async_copy(first, first_held, load_sem.at[0]),
        pltpu.make_async_copy(trailing, trailing_held, load_sem.at[1]),
        pltpu.make_async_copy(upper_one, one_held, load_sem.at[2]),
    ]
    for load in loads:
        load.start()
    group = summed.shape[0]
    rows = size // group
    gram = jnp.concatenate([summed[p, :rows] for p in range(group)], axis=0)
    cross = jnp.concatenate([summed[p, rows:] for p in range(group)], axis=0)
    uppers, inverses = factor([gram[h : h + 8] for h in range(0, size, 8)])
    inv = jnp.concatenate(inverses, axis=0)
    up = jnp.concatenate(uppers, axis=0)
    mixed = exact(cross, inv, NT)
    coupling_held[...] = mixed
    both = jnp.concatenate([inv * scale, exact(mixed, inv, NN)], axis=0)
    high, low = terms(both, 2)
    left = jnp.concatenate([low, low, high, high], axis=1)
    chunk = chunk_of(width, 512)
    stores = [pltpu.make_async_copy(coupling_held, coupling, load_sem.at[3])]
    stores[0].start()
    for load in loads:
        load.wait()
    upper_held[...] = exact(up, one_held[...], NN) * (1.0 / scale)
    stores.append(pltpu.make_async_copy(upper_held, upper, load_sem.at[4]))
    stores[-1].start()
    for i in range(width // chunk):
        at = pl.ds(i * chunk, chunk)
        high, low = terms(first_held[:, at], 2)
        out = stacked(left, jnp.concatenate([low, high, low, high], axis=0), NN)
        basis_held[:, at] = out[:size]
        updated_held[:, at] = trailing_held[:, at] - out[size:]
        for place, (src, dst) in enumerate(((basis_held, basis), (updated_held, updated))):
            stores.append(pltpu.make_async_copy(src.at[:, at], dst.at[:, at], store_sem.at[place, i]))
            stores[-1].start()
    for store in stores:
        store.wait()


def shards(sizes, panel, trailing):
    size, width = panel.shape
    trail = trailing.shape[0]
    nx, ny, nz = sizes
    group = nx * ny
    rows, less = size // group, trail // group
    f32 = jnp.float32
    scale = float(width * group * nz) ** 0.5

    def params(identity=None, mebibytes=53):
        return pltpu.CompilerParams(
            collective_id=identity, has_side_effects=identity is not None, vmem_limit_bytes=mebibytes * 2**20
        )

    first, upper_one, summed = pl.pallas_call(
        functools.partial(reduce_kernel, sizes),
        out_shape=[
            jax.ShapeDtypeStruct((size, width), f32),
            jax.ShapeDtypeStruct((size, size), f32),
            jax.ShapeDtypeStruct((group, rows + less, size), f32),
        ],
        in_specs=[HBM, HBM],
        out_specs=[HBM, HBM, VMEM],
        scratch_shapes=[
            pltpu.VMEM((size, width), f32),
            pltpu.VMEM((trail, width), f32),
            pltpu.VMEM((size, width), f32),
            pltpu.SemaphoreType.DMA((4, width // chunk_of(width, 1024))),
            pltpu.VMEM((size, size), f32),
            pltpu.VMEM((group, rows, size), f32),
            *sum_scratch(sizes, rows, size),
            *sum_scratch(sizes, rows + less, size),
        ],
        compiler_params=params(0),
        name="reduce",
    )(panel, trailing)
    basis, upper, coupling_t, updated = pl.pallas_call(
        functools.partial(final_kernel, scale),
        out_shape=[
            jax.ShapeDtypeStruct((size, width), f32),
            jax.ShapeDtypeStruct((size, size), f32),
            jax.ShapeDtypeStruct((trail, size), f32),
            jax.ShapeDtypeStruct((trail, width), f32),
        ],
        in_specs=[VMEM, HBM, HBM, HBM],
        out_specs=[HBM] * 4,
        scratch_shapes=[
            pltpu.VMEM((size, width), f32),
            pltpu.VMEM((trail, width), f32),
            pltpu.VMEM((size, width), f32),
            pltpu.VMEM((trail, width), f32),
            pltpu.VMEM((size, size), f32),
            pltpu.VMEM((size, size), f32),
            pltpu.VMEM((trail, size), f32),
            pltpu.SemaphoreType.DMA((5,)),
            pltpu.SemaphoreType.DMA((2, width // chunk_of(width, 512))),
        ],
        compiler_params=params(),
        name="final",
    )(summed, upper_one, first, trailing)
    return basis, upper, coupling_t.T, updated


def solution(mesh):
    sizes = tuple(mesh.shape[name] for name in ("gx", "gy", "gz"))
    placed = P(None, ("gx", "gy", "gz"))
    return jax.shard_map(
        functools.partial(shards, sizes),
        mesh=mesh,
        in_specs=(placed, placed),
        out_specs=(placed, P(), P(), placed),
        check_vma=False,
    )
```

profile of v0, /device:TPU:0, one launch (start us, length us, event | category | flops | bytes accessed | tf_op | source)
XLA Modules:
  0.0 40.7 jit_solution(2273608505369922137)
XLA Ops:
  0.6 33.4 %reduce.1 = (f32[128,4096]{1,0:T(8,128)}, f32[128,128]{1,0:T(8,128)S(1)}, f32[8,24,128]{2,1,0:T(8,128)S(1)}) custom-call(f32[128,4096]{1,0:T(8,128)} %panel.1, f32[64,4096]{1,0:T(8,128)} %trailing.3), custom_call_target="tpu_custom_call" | custom-call | tf_op jit(solution)/shard_map/reduce/pallas_call | solution.py:279
  34.0 6.6 %final.1 = (f32[128,4096]{1,0:T(8,128)}, f32[128,128]{1,0:T(8,128)}, f32[64,128]{1,0:T(8,128)}, f32[64,4096]{1,0:T(8,128)}) custom-call(f32[8,24,128]{2,1,0:T(8,128)S(1)} %get-tuple-element.11.summed, f32[128,128]{1,0:T(8,128)S(1)} %get-tuple-element.12.upper_one, f32[128,4096]{1,0:T(8,128)} %get-tuple-element.13.first, f32[64,4096]{1,0:T(8,128)} %trailing.3), custom_call_target="tpu_custom_call" | custom-call | tf_op jit(solution)/shard_map/final/pallas_call | solution.py:301
where the time goes:
time: 40.8 us; the launch traced here: 40.7 us
  Pallas kernels  40 us (98%)
  between operations  0.64 us (2%)
    pallas_call x1, Pallas kernels, shards(): pl.pallas_call(functools.partial(reduce_kernel, sizes), out_shape=[jax.Sh...  33.4 us
    pallas_call x1, Pallas kernels, shards(): pl.pallas_call(functools.partial(final_kernel, scale), out_shape=[jax.Sha...  6.62 us

commit v1 on v0

v1 whole, which is shorter than its diff:
```python
import functools

import jax
import jax.numpy as jnp
from jax import lax
from jax.experimental import pallas as pl
from jax.experimental.pallas import tpu as pltpu
from jax.sharding import PartitionSpec as P

MESH = pl.DeviceIdType.MESH
NT = (((1,), (1,)), ((), ()))
NN = (((1,), (0,)), ((), ()))
VMEM = pl.BlockSpec(memory_space=pltpu.VMEM)
HBM = pl.BlockSpec(memory_space=pltpu.HBM)


def dot(left, right, dims):
    return lax.dot_general(left, right, dims, preferred_element_type=jnp.float32)


def terms(value, count):
    found = []
    for _ in range(count):
        term = value.astype(jnp.bfloat16)
        found.append(term)
        value = value - term.astype(jnp.float32)
    return found


def left_terms(value):
    one, two, three = terms(value, 3)
    return jnp.concatenate([three, one, two, two, one, one], axis=1)


def right_terms(value, axis):
    one, two, three = terms(value, 3)
    return jnp.concatenate([one, three, two, one, two, one], axis=axis)


def product(left, right, dims):
    return dot(left_terms(left), right_terms(right, 1 if dims is NT else 0), dims)


def slices(value):
    top = jnp.max(jnp.abs(value), axis=1, keepdims=True) * 2.0**17
    high = (value + top) - top
    rest = value - high
    top = top * 2.0**-9
    middle = (rest + top) - top
    return high.astype(jnp.bfloat16), middle.astype(jnp.bfloat16), (rest - middle).astype(jnp.bfloat16)


def two_sum(one, two):
    total = one + two
    added = total - one
    return total, (one - (total - added)) + (two - added)


def factor(tiles):
    size = tiles[0].shape[1]
    lane = lax.broadcasted_iota(jnp.int32, (1, size), 1)
    row_in_tile = lax.broadcasted_iota(jnp.int32, (8, 1), 0)
    lanes = lax.broadcasted_iota(jnp.int32, (8, size), 1)
    tiles = list(tiles)
    for at in range(len(tiles)):
        first = 8 * at
        inside = (lane >= first) & (lane < first + 8)
        columns = {h: [jnp.broadcast_to(tiles[h][:, first + j : first + j + 1], (8, size)) for j in range(8)] for h in range(at, len(tiles))}
        for h in range(at + 1, len(tiles)):
            tiles[h] = jnp.where(inside, 0.0, tiles[h])
        for r in range(8):
            k = first + r
            row = tiles[at][r : r + 1, :]
            unit = jnp.where(lane == k, 1.0, row)
            behind = jnp.where(inside & (lane > k), 0.0, unit)
            pivots = [columns[at][j][r : r + 1, :] for j in range(8)]
            over = 1.0 / pivots[r]
            for h in range(at, len(tiles)):
                if h == at and r == 7:
                    continue
                times = columns[h][r] * over
                for j in range(r + 1, 8):
                    columns[h][j] = columns[h][j] - times * pivots[j]
                if h == at:
                    below = row_in_tile > r
                    tiles[h] = jnp.where(below, jnp.where(lanes == k, 0.0, tiles[h]) - times * unit, tiles[h])
                else:
                    tiles[h] = tiles[h] - times * behind
    uppers, inverses = [], []
    for h, tile in enumerate(tiles):
        rows = row_in_tile + 8 * h
        pivot = jnp.sum(jnp.where(lanes == rows, tile, 0.0), axis=1, keepdims=True)
        root = jnp.sqrt(pivot)
        over = 1.0 / root
        uppers.append(jnp.where(lanes > rows, tile * over, jnp.where(lanes == rows, root, 0.0)))
        inverses.append(jnp.where(lanes < rows, tile * over, jnp.where(lanes == rows, over, 0.0)))
    return uppers, inverses


def greet(sizes):
    nx, ny, nz = sizes
    gx, gy, gz = lax.axis_index("gx"), lax.axis_index("gy"), lax.axis_index("gz")
    barrier = pltpu.get_barrier_semaphore()
    me = gx * ny + gy
    for step in range(1, nx * ny):
        peer = lax.rem(me + step, nx * ny)
        pl.semaphore_signal(barrier, inc=1, device_id=(peer // ny, lax.rem(peer, ny), gz), device_id_type=MESH)
    for step in range(1, nz):
        pl.semaphore_signal(barrier, inc=1, device_id=(gx, gy, lax.rem(gz + step, nz)), device_id_type=MESH)


class Exchange:
    def __init__(self, sizes, send, landed, column, gathered, send_sem, recv_sem):
        nx, ny, nz = sizes
        self.nz, self.group = nz, nx * ny
        self.send, self.landed, self.column, self.gathered = send, landed, column, gathered
        gx, gy, gz = lax.axis_index("gx"), lax.axis_index("gy"), lax.axis_index("gz")
        group = self.group
        self.me, self.gz = gx * ny + gy, gz
        me = self.me

        def copy(src, dst, at, device):
            return pltpu.make_async_remote_copy(
                src_ref=src, dst_ref=dst, send_sem=send_sem.at[at], recv_sem=recv_sem.at[at], device_id=device, device_id_type=MESH
            )

        def in_plane(step):
            peer = lax.rem(me + step, group)
            return peer, (peer // ny, lax.rem(peer, ny), gz)

        self.out, self.back = [], []
        for step in range(1, group):
            peer, device = in_plane(step)
            self.out.append(copy(send.at[peer], landed.at[step], step, device))
            self.back.append(copy(gathered.at[me], gathered.at[me], group + nz + step, device))
        self.along = [
            copy(column.at[gz], column.at[gz], group + step, (gx, gy, lax.rem(gz + step, nz))) for step in range(1, nz)
        ]

    def parts(self):
        yield self.send[self.me]
        for step in range(1, self.group):
            self.out[step - 1].wait_recv()
            yield self.landed[step]

    def columns(self):
        for copy in self.along:
            copy.wait_recv()
        for z in range(self.nz):
            yield self.column[z]

    def finish(self):
        for copy in self.back:
            copy.wait_recv()

    def drain(self):
        for copy in self.out + self.along + self.back:
            copy.wait_send()


def start(copies):
    for copy in copies:
        copy.start()


def sum_pairs(values):
    total, lost = None, None
    for value in values:
        if total is None:
            total = value
        else:
            total, off = two_sum(total, value)
            lost = off if lost is None else lost + off
    return total, jnp.zeros_like(total) if lost is None else lost


def sum_plain(values):
    total = None
    for value in values:
        total = value if total is None else total + value
    return total


def exchange_scratch(sizes, rows, size):
    nx, ny, nz = sizes
    group = nx * ny
    return [
        pltpu.VMEM((group, rows, size), jnp.float32),
        pltpu.VMEM((group, rows, size), jnp.float32),
        pltpu.VMEM((nz, rows, size), jnp.float32),
        pltpu.VMEM((group, rows, size), jnp.float32),
        pltpu.SemaphoreType.DMA((2 * group + nz,)),
        pltpu.SemaphoreType.DMA((2 * group + nz,)),
    ]


def chunk_of(width, most):
    return most if width % most == 0 else width


def reduce_kernel(sizes, panel, trailing, gram_out, rest_out, upper_out, inverse_out, panel_held, trailing_held, sliced, move_sem, *scratch):
    size, width = panel.shape
    trail = trailing.shape[0]
    group = sizes[0] * sizes[1]
    rows, less = size // group, trail // group
    chunk = chunk_of(width, 1024)
    steps = width // chunk
    greet(sizes)
    loads, more = [], []
    for i in range(steps):
        at = pl.ds(i * chunk, chunk)
        loads.append(pltpu.make_async_copy(panel.at[:, at], panel_held.at[:, at], move_sem.at[0, i]))
        loads[-1].start()
    for i in range(steps):
        at = pl.ds(i * chunk, chunk)
        more.append(pltpu.make_async_copy(trailing.at[:, at], trailing_held.at[:, at], move_sem.at[1, i]))
        more[-1].start()
    zero = jnp.zeros((size, size), jnp.float32)
    gram, lost, mixed, small = zero, zero, zero, zero
    for i in range(steps):
        loads[i].wait()
        at = slice(i * chunk, (i + 1) * chunk)
        high, middle, low = slices(panel_held[:, at])
        pair = jnp.concatenate([high, middle], axis=0)
        sliced[: 2 * size, at] = pair
        sliced[2 * size :, at] = low
        first = dot(pair, pair, NT)
        second = dot(low, pair, NT)
        gram, off = two_sum(gram, first[:size, :size])
        lost = lost + off
        mixed = mixed + (first[:size, size:] + (second[:, :size] + second[:, size:]))
        small = small + (first[size:, size:] + dot(low, low, NT))
    gram, off = two_sum(gram, small + (mixed + mixed.T))
    lost = lost + off
    heads = Exchange(sizes, *scratch[:6])
    tails = Exchange(sizes, *scratch[6:])
    for p in range(group):
        heads.send[p] = gram[p * rows : (p + 1) * rows]
    pl.semaphore_wait(pltpu.get_barrier_semaphore(), group - 1 + sizes[2] - 1)
    start(heads.out)
    cross = jnp.zeros((trail, size), jnp.float32)
    for i in range(steps):
        more[i].wait()
        at = slice(i * chunk, (i + 1) * chunk)
        found = dot(jnp.concatenate(terms(trailing_held[:, at], 2), axis=0), sliced[:, at], NT)
        found = found[:trail] + found[trail:]
        cross = cross + (found[:, :size] + (found[:, size : 2 * size] + found[:, 2 * size :]))
    for p in range(group):
        tails.send[p, :rows] = lost[p * rows : (p + 1) * rows]
        tails.send[p, rows:] = cross[p * less : (p + 1) * less]
    start(tails.out)
    total, lost_out = sum_pairs(heads.parts())
    heads.column[heads.gz] = total
    start(heads.along)
    part = sum_plain(tails.parts())
    tails.column[tails.gz, :rows] = part[:rows] + lost_out
    tails.column[tails.gz, rows:] = part[rows:]
    total, lost_along = sum_pairs(heads.columns())
    heads.gathered[heads.me] = total
    start(heads.back)
    start(tails.along)
    part = sum_plain(tails.columns())
    tails.gathered[tails.me, :rows] = part[:rows] + lost_along
    tails.gathered[tails.me, rows:] = part[rows:]
    heads.finish()
    start(tails.back)
    gram = jnp.concatenate([heads.gathered[p] for p in range(group)], axis=0)
    uppers, inverses = factor([gram[h : h + 8] for h in range(0, size, 8)])
    for h in range(len(uppers)):
        upper_out[8 * h : 8 * h + 8] = uppers[h]
        inverse_out[8 * h : 8 * h + 8] = inverses[h]
    gram_out[...] = gram
    tails.finish()
    for p in range(group):
        rest_out[p] = tails.gathered[p]
    heads.drain()
    tails.drain()


def refine(gram, lost, cross, first_upper, inverse):
    size = gram.shape[0]
    row = lax.broadcasted_iota(jnp.int32, (size, size), 0)
    lane = lax.broadcasted_iota(jnp.int32, (size, size), 1)
    high, middle, low = slices(first_upper.T)
    pair = jnp.concatenate([high, middle], axis=0)
    first = dot(pair, pair, NT)
    second = dot(low, pair, NT)
    mixed = first[:size, size:] + (second[:, :size] + second[:, size:])
    small = (first[size:, size:] + dot(low, low, NT)) + (mixed + mixed.T)
    off, lower_off = two_sum(gram, -first[:size, :size])
    off = (off - small) + (lower_off + lost)
    lower = (high.astype(jnp.float32) + middle.astype(jnp.float32)) + low.astype(jnp.float32)
    both = product(inverse, jnp.concatenate([lower, off], axis=1), NN)
    second_gram = product(both, jnp.concatenate([both[:, :size], inverse], axis=1), NT)

    def correction(value):
        return jnp.where(row > lane, -value, jnp.where(row == lane, 1.5 - 0.5 * value, 0.0))

    step = correction(second_gram)
    inverse = product(step, inverse, NN)
    step = correction(product(product(step, second_gram, NN), step, NT))
    inverse = product(step, inverse, NN)
    mixed = product(cross, inverse, NT)
    upper = product(inverse, gram, NN) + product(inverse, lost, NN)
    return inverse, product(mixed, inverse, NN), jnp.where(row <= lane, upper, 0.0), mixed


def final_kernel(scale, gram, rest, first_upper, inverse, panel, trailing, basis, upper, coupling, updated, panel_held, trailing_held, basis_held, updated_held, upper_held, coupling_held, load_sem, store_sem):
    size, width = panel.shape
    trail = trailing.shape[0]
    chunk = chunk_of(width, 512)
    loads = [
        pltpu.make_async_copy(panel, panel_held, load_sem.at[0]),
        pltpu.make_async_copy(trailing, trailing_held, load_sem.at[1]),
    ]
    start(loads)
    group = rest.shape[0]
    rows = size // group
    lost = jnp.concatenate([rest[p, :rows] for p in range(group)], axis=0)
    cross = jnp.concatenate([rest[p, rows:] for p in range(group)], axis=0)
    whole, projected, total, mixed = refine(gram[...], lost, cross, first_upper[...], inverse[...])
    coupling_held[...] = mixed
    upper_held[...] = total * (1.0 / scale)
    stores = [
        pltpu.make_async_copy(coupling_held, coupling, load_sem.at[2]),
        pltpu.make_async_copy(upper_held, upper, load_sem.at[3]),
    ]
    start(stores)
    left = left_terms(jnp.concatenate([whole * scale, projected], axis=0))
    for load in loads:
        load.wait()
    for i in range(width // chunk):
        at = pl.ds(i * chunk, chunk)
        out = dot(left, right_terms(panel_held[:, at], 0), NN)
        basis_held[:, at] = out[:size]
        updated_held[:, at] = trailing_held[:, at] - out[size:]
        for place, (src, dst) in enumerate(((basis_held, basis), (updated_held, updated))):
            stores.append(pltpu.make_async_copy(src.at[:, at], dst.at[:, at], store_sem.at[place, i]))
            stores[-1].start()
    for store in stores:
        store.wait()


def shards(sizes, panel, trailing):
    size, width = panel.shape
    trail = trailing.shape[0]
    nx, ny, nz = sizes
    group = nx * ny
    rows, less = size // group, trail // group
    f32 = jnp.float32
    scale = float(width * group * nz) ** 0.5

    def params(identity=None, mebibytes=53):
        return pltpu.CompilerParams(
            collective_id=identity, has_side_effects=identity is not None, vmem_limit_bytes=mebibytes * 2**20
        )

    square = jax.ShapeDtypeStruct((size, size), f32)
    gram, rest, first_upper, inverse = pl.pallas_call(
        functools.partial(reduce_kernel, sizes),
        out_shape=[square, jax.ShapeDtypeStruct((group, rows + less, size), f32), square, square],
        in_specs=[HBM, HBM],
        out_specs=[VMEM] * 4,
        scratch_shapes=[
            pltpu.VMEM((size, width), f32),
            pltpu.VMEM((trail, width), f32),
            pltpu.VMEM((3 * size, width), jnp.bfloat16),
            pltpu.SemaphoreType.DMA((2, width // chunk_of(width, 1024))),
            *exchange_scratch(sizes, rows, size),
            *exchange_scratch(sizes, rows + less, size),
        ],
        compiler_params=params(0),
        name="reduce",
    )(panel, trailing)
    basis, upper, coupling_t, updated = pl.pallas_call(
        functools.partial(final_kernel, scale),
        out_shape=[
            jax.ShapeDtypeStruct((size, width), f32),
            square,
            jax.ShapeDtypeStruct((trail, size), f32),
            jax.ShapeDtypeStruct((trail, width), f32),
        ],
        in_specs=[VMEM] * 4 + [HBM] * 2,
        out_specs=[HBM] * 4,
        scratch_shapes=[
            pltpu.VMEM((size, width), f32),
            pltpu.VMEM((trail, width), f32),
            pltpu.VMEM((size, width), f32),
            pltpu.VMEM((trail, width), f32),
            pltpu.VMEM((size, size), f32),
            pltpu.VMEM((trail, size), f32),
            pltpu.SemaphoreType.DMA((4,)),
            pltpu.SemaphoreType.DMA((2, width // chunk_of(width, 512))),
        ],
        compiler_params=params(),
        name="final",
    )(gram, rest, first_upper, inverse, panel, trailing)
    return basis, upper, coupling_t.T, updated


def solution(mesh):
    sizes = tuple(mesh.shape[name] for name in ("gx", "gy", "gz"))
    placed = P(None, ("gx", "gy", "gz"))
    return jax.shard_map(
        functools.partial(shards, sizes),
        mesh=mesh,
        in_specs=(placed, placed),
        out_specs=(placed, P(), P(), placed),
        check_vma=False,
    )
```

time: 40.8 us -> 29 us (0.71)
  Pallas kernels: 40 us -> 28.2 us
    pallas_call x1, Pallas kernels: 33.4 us -> 22.3 us  [shards(): pl.pallas_call(functools.partial(reduce_kernel, sizes), out_shape=[square...]
    pallas_call x1, Pallas kernels: 6.62 us -> 5.9 us  [shards(): pl.pallas_call(functools.partial(final_kernel, scale), out_shape=[jax.Sha...]
where the time goes in v1:
time: 29 us; the launch traced here: 28.8 us
  Pallas kernels  28.2 us (97%)
  between operations  0.64 us (2%)
    pallas_call x1, Pallas kernels, shards(): pl.pallas_call(functools.partial(reduce_kernel, sizes), out_shape=[square...  22.3 us
    pallas_call x1, Pallas kernels, shards(): pl.pallas_call(functools.partial(final_kernel, scale), out_shape=[jax.Sha...  5.9 us

profile of v1, /device:TPU:0, one launch (start us, length us, event | category | flops | bytes accessed | tf_op | source)
XLA Modules:
  0.0 28.8 jit_solution(8034006324864348706)
XLA Ops:
  0.6 22.3 %reduce.1 = (f32[128,128]{1,0:T(8,128)S(1)}, f32[8,24,128]{2,1,0:T(8,128)S(1)}, f32[128,128]{1,0:T(8,128)S(1)}, f32[128,128]{1,0:T(8,128)S(1)}) custom-call(f32[128,4096]{1,0:T(8,128)} %panel.3, f32[64,4096]{1,0:T(8,128)} %trailing.3), custom_call_target="tpu_custom_call" | custom-call | tf_op jit(solution)/shard_map/reduce/pallas_call | solution.py:359
  22.9 5.9 %final.1 = (f32[128,4096]{1,0:T(8,128)}, f32[128,128]{1,0:T(8,128)}, f32[64,128]{1,0:T(8,128)}, f32[64,4096]{1,0:T(8,128)}) custom-call(f32[128,128]{1,0:T(8,128)S(1)} %get-tuple-element.12.gram, f32[8,24,128]{2,1,0:T(8,128)S(1)} %get-tuple-element.13.rest, f32[128,128]{1,0:T(8,128)S(1)} %get-tuple-element.14.first_upper, ...), custom_call_target="tpu_custom_call" | custom-call | tf_op jit(solution)/shard_map/final/pallas_call | solution.py:375

commit v2 on v1

v2 whole, which is shorter than its diff:
```python
import functools

import jax
import jax.numpy as jnp
from jax import lax
from jax.experimental import pallas as pl
from jax.experimental.pallas import tpu as pltpu
from jax.sharding import PartitionSpec as P

MESH = pl.DeviceIdType.MESH
NT = (((1,), (1,)), ((), ()))
NN = (((1,), (0,)), ((), ()))
TN = (((0,), (0,)), ((), ()))
VMEM = pl.BlockSpec(memory_space=pltpu.VMEM)
HBM = pl.BlockSpec(memory_space=pltpu.HBM)


def dot(left, right, dims):
    return lax.dot_general(left, right, dims, preferred_element_type=jnp.float32)


def terms(value, count):
    found = []
    for _ in range(count):
        term = value.astype(jnp.bfloat16)
        found.append(term)
        value = value - term.astype(jnp.float32)
    return found


def left_terms(value):
    one, two, three = terms(value, 3)
    return jnp.concatenate([three, one, two, two, one, one], axis=1)


def right_terms(value, axis):
    one, two, three = terms(value, 3)
    return jnp.concatenate([one, three, two, one, two, one], axis=axis)


def product(left, right, dims):
    return dot(left_terms(left), right_terms(right, 1 if dims is NT else 0), dims)


def slices(value):
    top = jnp.max(jnp.abs(value), axis=1, keepdims=True) * 2.0**17
    high = (value + top) - top
    rest = value - high
    top = top * 2.0**-9
    middle = (rest + top) - top
    return high.astype(jnp.bfloat16), middle.astype(jnp.bfloat16), (rest - middle).astype(jnp.bfloat16)


def two_sum(one, two):
    total = one + two
    added = total - one
    return total, (one - (total - added)) + (two - added)


def factor(tiles, depth=8):
    size = tiles[0].shape[1]
    shape = (8, size)
    lanes = lax.broadcasted_iota(jnp.int32, shape, 1)
    row_in_tile = lax.broadcasted_iota(jnp.int32, shape, 0)
    tiles = list(tiles)
    count = len(tiles)

    def across(tile, column):
        return jnp.broadcast_to(jnp.sum(jnp.where(lanes == column, tile, 0.0), axis=1, keepdims=True), shape)

    def down(tile, row):
        return jnp.broadcast_to(tile[row : row + 1, :], shape)

    for start in range(0, count, depth):
        stop = min(start + depth, count)
        own = [across(tiles[start], 8 * start + j) for j in range(8)]
        scales = []
        for at in range(start, stop):
            first = 8 * at
            inside = (lanes >= first) & (lanes < first + 8)
            raw = list(tiles)
            columns = after = None
            if at + 1 < stop:
                columns = [across(raw[at + 1], first + j) for j in range(8)]
                after = [across(raw[at + 1], first + 8 + j) for j in range(8)]
            tile = tiles[at]
            scaled, ratios, scale = [], [], None
            for h in range(at + 1, stop):
                tiles[h] = jnp.where(inside, 0.0, tiles[h])
            for r in range(8):
                k = first + r
                pivots = {j: down(own[j], r) for j in range(r, 8)}
                over = 1.0 / pivots[r]
                scale = over if scale is None else jnp.where(row_in_tile == r, over, scale)
                ratios.append({j: pivots[j] * over for j in range(r + 1, 8)})
                unit = jnp.where(lanes == k, 1.0, down(tile, r))
                scaled.append(jnp.where(inside & (lanes > k), 0.0, unit) * over)
                if r < 7:
                    for j in range(r + 1, 8):
                        own[j] = own[j] - own[r] * ratios[r][j]
                    below = jnp.where(lanes == k, 0.0, tile) - (own[r] * over) * unit
                    tile = jnp.where(row_in_tile > r, below, tile)
                if after is not None:
                    column = columns[r]
                    for j in range(r + 1, 8):
                        columns[j] = columns[j] - column * ratios[r][j]
                    tiles[at + 1] = tiles[at + 1] - column * scaled[r]
                    times = column * over
                    for j in range(8):
                        after[j] = after[j] - times * down(column, j)
            tiles[at] = tile
            scales.append(scale)
            for h in range(at + 2, stop):
                columns = [across(raw[h], first + j) for j in range(8)]
                total = tiles[h]
                for r in range(8):
                    column = columns[r]
                    for j in range(r + 1, 8):
                        columns[j] = columns[j] - column * ratios[r][j]
                    total = total - column * scaled[r]
                tiles[h] = total
            own = after
        if stop < count:
            inner = (lanes >= 8 * start) & (lanes < 8 * stop)
            left = jnp.concatenate(tiles[start:stop], axis=0)
            right = []
            for h in range(start, stop):
                rows = row_in_tile + 8 * h
                right.append(jnp.where(lanes == rows, 1.0, jnp.where(inner & (lanes > rows), 0.0, tiles[h])) * scales[h - start])
            b1, b2, b3 = terms(jnp.concatenate(right, axis=0), 3)
            a1, a2, a3 = terms(left, 3)
            a = jnp.concatenate([a3, a1, a2, a2, a1, a1], axis=0)
            update = dot(a, jnp.concatenate([b1, b3, b2, b1, b2, b1], axis=0), TN)
            for h in range(stop, count):
                tiles[h] = jnp.where(inner, 0.0, tiles[h]) - update[8 * h : 8 * h + 8]
    uppers, inverses = [], []
    for h, tile in enumerate(tiles):
        rows = row_in_tile + 8 * h
        pivot = jnp.sum(jnp.where(lanes == rows, tile, 0.0), axis=1, keepdims=True)
        root = jnp.sqrt(pivot)
        over = 1.0 / root
        uppers.append(jnp.where(lanes > rows, tile * over, jnp.where(lanes == rows, root, 0.0)))
        inverses.append(jnp.where(lanes < rows, tile * over, jnp.where(lanes == rows, over, 0.0)))
    return uppers, inverses


def greet(sizes):
    nx, ny, nz = sizes
    gx, gy, gz = lax.axis_index("gx"), lax.axis_index("gy"), lax.axis_index("gz")
    barrier = pltpu.get_barrier_semaphore()
    me = gx * ny + gy
    for step in range(1, nx * ny):
        peer = lax.rem(me + step, nx * ny)
        pl.semaphore_signal(barrier, inc=1, device_id=(peer // ny, lax.rem(peer, ny), gz), device_id_type=MESH)
    for step in range(1, nz):
        pl.semaphore_signal(barrier, inc=1, device_id=(gx, gy, lax.rem(gz + step, nz)), device_id_type=MESH)


class Exchange:
    def __init__(self, sizes, send, landed, column, gathered, send_sem, recv_sem):
        nx, ny, nz = sizes
        self.nz, self.group = nz, nx * ny
        self.send, self.landed, self.column, self.gathered = send, landed, column, gathered
        gx, gy, gz = lax.axis_index("gx"), lax.axis_index("gy"), lax.axis_index("gz")
        group = self.group
        self.me, self.gz = gx * ny + gy, gz
        me = self.me

        def copy(src, dst, at, device):
            return pltpu.make_async_remote_copy(
                src_ref=src, dst_ref=dst, send_sem=send_sem.at[at], recv_sem=recv_sem.at[at], device_id=device, device_id_type=MESH
            )

        def in_plane(step):
            peer = lax.rem(me + step, group)
            return peer, (peer // ny, lax.rem(peer, ny), gz)

        self.out, self.back = [], []
        for step in range(1, group):
            peer, device = in_plane(step)
            self.out.append(copy(send.at[peer], landed.at[step], step, device))
            self.back.append(copy(gathered.at[me], gathered.at[me], group + nz + step, device))
        self.along = [
            copy(column.at[gz], column.at[gz], group + step, (gx, gy, lax.rem(gz + step, nz))) for step in range(1, nz)
        ]

    def parts(self):
        yield self.send[self.me]
        for step in range(1, self.group):
            self.out[step - 1].wait_recv()
            yield self.landed[step]

    def columns(self):
        for copy in self.along:
            copy.wait_recv()
        for z in range(self.nz):
            yield self.column[z]

    def finish(self):
        for copy in self.back:
            copy.wait_recv()

    def drain(self):
        for copy in self.out + self.along + self.back:
            copy.wait_send()


def start(copies):
    for copy in copies:
        copy.start()


def sum_pairs(values):
    total, lost = None, None
    for value in values:
        if total is None:
            total = value
        else:
            total, off = two_sum(total, value)
            lost = off if lost is None else lost + off
    return total, jnp.zeros_like(total) if lost is None else lost


def sum_plain(values):
    total = None
    for value in values:
        total = value if total is None else total + value
    return total


def exchange_scratch(sizes, rows, size):
    nx, ny, nz = sizes
    group = nx * ny
    return [
        pltpu.VMEM((group, rows, size), jnp.float32),
        pltpu.VMEM((group, rows, size), jnp.float32),
        pltpu.VMEM((nz, rows, size), jnp.float32),
        pltpu.VMEM((group, rows, size), jnp.float32),
        pltpu.SemaphoreType.DMA((2 * group + nz,)),
        pltpu.SemaphoreType.DMA((2 * group + nz,)),
    ]


def chunk_of(width, most):
    return most if width % most == 0 else width


def reduce_kernel(sizes, panel, trailing, gram_out, rest_out, off_out, product_out, inverse_out, pieces, trailing_held, panel_held, sliced, move_sem, *scratch):
    size, width = panel.shape
    trail = trailing.shape[0]
    group = sizes[0] * sizes[1]
    rows, less = size // group, trail // group
    chunk = chunk_of(width, 512)
    steps = width // chunk
    spans = [slice(i * chunk, (i + 1) * chunk) for i in range(steps)]
    loads = []
    for i in range(steps):
        at = pl.ds(i * chunk, chunk)
        loads.append(pltpu.make_async_copy(panel.at[:, at], panel_held.at[:, at], move_sem.at[i]))
    loads.append(pltpu.make_async_copy(trailing, trailing_held, move_sem.at[steps]))
    start(loads)
    greet(sizes)
    zero = jnp.zeros((size, size), jnp.float32)
    gram, lost, mixed, small = zero, zero, zero, zero
    for i in range(steps + 1):
        if i < steps:
            loads[i].wait()
            high, middle, low = slices(panel_held[:, spans[i]])
            sliced[:size, spans[i]] = high
            sliced[size : 2 * size, spans[i]] = middle
            sliced[2 * size :, spans[i]] = low
        if i > 0:
            pair = sliced[: 2 * size, spans[i - 1]]
            first = dot(pair, pair, NT)
            second = dot(sliced[2 * size :, spans[i - 1]], pair, NT)
            gram, off = two_sum(gram, first[:size, :size])
            lost = lost + off
            mixed = mixed + (first[:size, size:] + (second[:, :size] + second[:, size:]))
            small = small + first[size:, size:]
    gram, off = two_sum(gram, small + (mixed + mixed.T))
    lost = lost + off
    heads = Exchange(sizes, *scratch[:6])
    tails = Exchange(sizes, *scratch[6:])
    for p in range(group):
        heads.send[p] = gram[p * rows : (p + 1) * rows]
    pl.semaphore_wait(pltpu.get_barrier_semaphore(), group - 1 + sizes[2] - 1)
    start(heads.out)
    loads[steps].wait()
    cross = jnp.zeros((trail, size), jnp.float32)
    for span in spans:
        both = jnp.concatenate(terms(trailing_held[:, span], 2), axis=0)
        low = sliced[2 * size :, span]
        found = dot(both, sliced[: 2 * size, span], NT)
        last = dot(jnp.concatenate([low, both], axis=0), low, NT)
        found = found[:, :size] + (found[:, size:] + last[size:])
        cross = cross + (found[:trail] + found[trail:])
        lost = lost + last[:size]
    for p in range(group):
        tails.send[p, :rows] = lost[p * rows : (p + 1) * rows]
        tails.send[p, rows:] = cross[p * less : (p + 1) * less]
    total, lost_out = sum_pairs(heads.parts())
    heads.column[heads.gz] = total
    start(heads.along)
    start(tails.out)
    for span in spans[: steps // 2]:
        for t, term in enumerate(terms(panel_held[:, span], 3)):
            pieces[t * size : (t + 1) * size, span] = term
    total, lost_along = sum_pairs(heads.columns())
    heads.gathered[heads.me] = total
    start(heads.back)
    part = sum_plain(tails.parts())
    tails.column[tails.gz, :rows] = part[:rows] + lost_out
    tails.column[tails.gz, rows:] = part[rows:]
    start(tails.along)
    for span in spans[steps // 2 :]:
        for t, term in enumerate(terms(panel_held[:, span], 3)):
            pieces[t * size : (t + 1) * size, span] = term
    heads.finish()
    part = sum_plain(tails.columns())
    tails.gathered[tails.me, :rows] = part[:rows] + lost_along
    tails.gathered[tails.me, rows:] = part[rows:]
    start(tails.back)
    gram = jnp.concatenate([heads.gathered[p] for p in range(group)], axis=0)
    uppers, inverses = factor([gram[h : h + 8] for h in range(0, size, 8)])
    inverse = jnp.concatenate(inverses, axis=0)
    gram_out[...] = gram
    inverse_out[...] = inverse
    off, turned = departure(gram, jnp.concatenate(uppers, axis=0), inverse)
    off_out[...] = off
    product_out[...] = turned
    tails.finish()
    for p in range(group):
        rest_out[p] = tails.gathered[p]
    heads.drain()
    tails.drain()


def departure(gram, upper, inverse):
    size = gram.shape[0]
    high, middle, low = slices(upper.T)
    pair = jnp.concatenate([high, middle], axis=0)
    first = dot(pair, pair, NT)
    second = dot(low, pair, NT)
    mixed = first[:size, size:] + (second[:, :size] + second[:, size:])
    small = (first[size:, size:] + dot(low, low, NT)) + (mixed + mixed.T)
    off, lower_off = two_sum(gram, -first[:size, :size])
    lower = (high.astype(jnp.float32) + middle.astype(jnp.float32)) + low.astype(jnp.float32)
    return (off - small) + lower_off, product(inverse, lower, NN)


def refine(off, turned, inverse):
    size = off.shape[0]
    row = lax.broadcasted_iota(jnp.int32, (size, size), 0)
    lane = lax.broadcasted_iota(jnp.int32, (size, size), 1)

    def correction(value):
        return jnp.where(row > lane, -value, jnp.where(row == lane, 1.5 - 0.5 * value, 0.0))

    moved = product(inverse, off, NN)
    second_gram = product(jnp.concatenate([turned, moved], axis=1), jnp.concatenate([turned, inverse], axis=1), NT)
    step = correction(second_gram)
    inverse = product(step, inverse, NN)
    step = correction(product(product(step, second_gram, NN), step, NT))
    return product(step, inverse, NN)


def final_kernel(scale, gram, rest, off, turned, inverse, pieces, trailing, basis, upper, coupling, updated, basis_held, updated_held, upper_held, coupling_held, store_sem):
    size, width = basis.shape
    chunk = chunk_of(width, 512)
    steps = width // chunk
    group = rest.shape[0]
    rows = size // group
    lost = jnp.concatenate([rest[p, :rows] for p in range(group)], axis=0)
    cross = jnp.concatenate([rest[p, rows:] for p in range(group)], axis=0)
    whole = refine(off[...] + lost, turned[...], inverse[...])
    left = left_terms(whole * scale)
    mixed = product(cross, whole, NT)
    coupling_held[...] = mixed
    one, two = terms(mixed * (1.0 / scale), 2)
    back = jnp.concatenate([two, one, one], axis=1)
    stores = []

    def store(src, dst, place):
        stores.append(pltpu.make_async_copy(src, dst, store_sem.at[place]))
        stores[-1].start()

    for i in range(steps):
        span, at = slice(i * chunk, (i + 1) * chunk), pl.ds(i * chunk, chunk)
        one, two, three = (pieces[t * size : (t + 1) * size, span] for t in range(3))
        out = dot(left, jnp.concatenate([one, three, two, one, two, one], axis=0), NN)
        basis_held[:, span] = out
        store(basis_held.at[:, at], basis.at[:, at], 2 * i)
        one, two = terms(out, 2)
        updated_held[:, span] = trailing[:, span] - dot(back, jnp.concatenate([one, two, one], axis=0), NN)
        store(updated_held.at[:, at], updated.at[:, at], 2 * i + 1)
        if i == 0:
            row = lax.broadcasted_iota(jnp.int32, (size, size), 0)
            lane = lax.broadcasted_iota(jnp.int32, (size, size), 1)
            total = product(whole, gram[...], NN) + product(whole, lost, NN)
            upper_held[...] = jnp.where(row <= lane, total * (1.0 / scale), 0.0)
            store(coupling_held, coupling, 2 * steps)
            store(upper_held, upper, 2 * steps + 1)
    for copy in stores:
        copy.wait()


def shards(sizes, panel, trailing):
    size, width = panel.shape
    trail = trailing.shape[0]
    nx, ny, nz = sizes
    group = nx * ny
    rows, less = size // group, trail // group
    f32 = jnp.float32
    scale = float(width * group * nz) ** 0.5

    def params(identity=None, mebibytes=40):
        return pltpu.CompilerParams(
            collective_id=identity, has_side_effects=identity is not None, vmem_limit_bytes=mebibytes * 2**20
        )

    square = jax.ShapeDtypeStruct((size, size), f32)
    held = pl.pallas_call(
        functools.partial(reduce_kernel, sizes),
        out_shape=[
            square,
            jax.ShapeDtypeStruct((group, rows + less, size), f32),
            square,
            square,
            square,
            jax.ShapeDtypeStruct((3 * size, width), jnp.bfloat16),
            jax.ShapeDtypeStruct((trail, width), f32),
        ],
        in_specs=[HBM, HBM],
        out_specs=[VMEM] * 7,
        scratch_shapes=[
            pltpu.VMEM((size, width), f32),
            pltpu.VMEM((3 * size, width), jnp.bfloat16),
            pltpu.SemaphoreType.DMA((width // chunk_of(width, 512) + 1,)),
            *exchange_scratch(sizes, rows, size),
            *exchange_scratch(sizes, rows + less, size),
        ],
        compiler_params=params(0),
        name="reduce",
    )(pltpu.with_memory_space_constraint(panel, pltpu.HBM), pltpu.with_memory_space_constraint(trailing, pltpu.HBM))
    basis, upper, coupling_t, updated = pl.pallas_call(
        functools.partial(final_kernel, scale),
        out_shape=[
            jax.ShapeDtypeStruct((size, width), f32),
            square,
            jax.ShapeDtypeStruct((trail, size), f32),
            jax.ShapeDtypeStruct((trail, width), f32),
        ],
        in_specs=[VMEM] * 7,
        out_specs=[HBM] * 4,
        scratch_shapes=[
            pltpu.VMEM((size, width), f32),
            pltpu.VMEM((trail, width), f32),
            pltpu.VMEM((size, size), f32),
            pltpu.VMEM((trail, size), f32),
            pltpu.SemaphoreType.DMA((2 * (width // chunk_of(width, 512)) + 2,)),
        ],
        compiler_params=params(),
        name="final",
    )(*held)
    return basis, upper, coupling_t.T, updated


def solution(mesh):
    sizes = tuple(mesh.shape[name] for name in ("gx", "gy", "gz"))
    placed = P(None, ("gx", "gy", "gz"))
    return jax.shard_map(
        functools.partial(shards, sizes),
        mesh=mesh,
        in_specs=(placed, placed),
        out_specs=(placed, P(), P(), placed),
        check_vma=False,
    )
```

time: 29 us -> 27.5 us (0.948)
  Pallas kernels: 28.2 us -> 26.7 us
    pallas_call x1, Pallas kernels: 5.9 us -> 4.68 us  [shards(): pl.pallas_call(functools.partial(final_kernel, scale), out_shape=[jax.Sha...]
    pallas_call x1, Pallas kernels: 22.3 us -> 22 us  [shards(): pl.pallas_call(functools.partial(reduce_kernel, sizes), out_shape=[square...]
where the time goes in v2:
time: 27.5 us; the launch traced here: 27.3 us
  Pallas kernels  26.7 us (97%)
  between operations  0.64 us (2%)
    pallas_call x1, Pallas kernels, shards(): pl.pallas_call(functools.partial(reduce_kernel, sizes), out_shape=[square...  22 us
    pallas_call x1, Pallas kernels, shards(): pl.pallas_call(functools.partial(final_kernel, scale), out_shape=[jax.Sha...  4.68 us

profile of v2, /device:TPU:0, one launch (start us, length us, event | category | flops | bytes accessed | tf_op | source)
XLA Modules:
  0.0 27.3 jit_solution(5106261597505403270)
XLA Ops:
  0.6 22.0 %reduce.1 = (f32[128,128]{1,0:T(8,128)S(1)}, f32[8,24,128]{2,1,0:T(8,128)S(1)}, f32[128,128]{1,0:T(8,128)S(1)}, f32[128,128]{1,0:T(8,128)S(1)}, f32[128,128]{1,0...) custom-call(f32[128,4096]{1,0:T(8,128)} %panel.1, f32[64,4096]{1,0:T(8,128)} %trailing.1), custom_call_target="tpu_custom_call" | custom-call | tf_op jit(solution)/shard_map/reduce/pallas_call | solution.py:422
  22.6 4.7 %final.1 = (f32[128,4096]{1,0:T(8,128)}, f32[128,128]{1,0:T(8,128)}, f32[64,128]{1,0:T(8,128)}, f32[64,4096]{1,0:T(8,128)}) custom-call(f32[128,128]{1,0:T(8,128)S(1)} %get-tuple-element.15.gram, f32[8,24,128]{2,1,0:T(8,128)S(1)} %get-tuple-element.16.rest, f32[128,128]{1,0:T(8,128)S(1)} %get-tuple-element.17.off, f32[128,128]{1,0:T(8,128)S(1)} %get-tuple-element.18.turned, ...), custom_call_target="tpu_custom_call" | custom-call | tf_op jit(solution)/shard_map/final/pallas_call | solution.py:445

commit v3 on v2

--- a/solution.py
+++ b/solution.py
@@ -241,6 +241,11 @@
     ]
 
 
+def halves(span):
+    middle = (span.start + span.stop) // 2
+    return slice(span.start, middle), slice(middle, span.stop)
+
+
 def chunk_of(width, most):
     return most if width % most == 0 else width
 
@@ -250,7 +255,7 @@
     trail = trailing.shape[0]
     group = sizes[0] * sizes[1]
     rows, less = size // group, trail // group
-    chunk = chunk_of(width, 512)
+    chunk = chunk_of(width, 1024)
     steps = width // chunk
     spans = [slice(i * chunk, (i + 1) * chunk) for i in range(steps)]
     loads = []
@@ -265,18 +270,16 @@
     for i in range(steps + 1):
         if i < steps:
             loads[i].wait()
-            high, middle, low = slices(panel_held[:, spans[i]])
-            sliced[:size, spans[i]] = high
-            sliced[size : 2 * size, spans[i]] = middle
-            sliced[2 * size :, spans[i]] = low
+            for t in range(0, size, 16):
+                for place, part in enumerate(slices(panel_held[t : t + 16, spans[i]])):
+                    sliced[place * size + t : place * size + t + 16, spans[i]] = part
         if i > 0:
-            pair = sliced[: 2 * size, spans[i - 1]]
-            first = dot(pair, pair, NT)
-            second = dot(sliced[2 * size :, spans[i - 1]], pair, NT)
-            gram, off = two_sum(gram, first[:size, :size])
-            lost = lost + off
-            mixed = mixed + (first[:size, size:] + (second[:, :size] + second[:, size:]))
-            small = small + first[size:, size:]
+            for half in halves(spans[i - 1]):
+                found = dot(sliced[:, half], sliced[: 2 * size, half], NT)
+                gram, off = two_sum(gram, found[:size, :size])
+                lost = lost + off
+                mixed = mixed + (found[:size, size:] + (found[2 * size :, :size] + found[2 * size :, size:]))
+                small = small + found[size : 2 * size, size:]
     gram, off = two_sum(gram, small + (mixed + mixed.T))
     lost = lost + off
     heads = Exchange(sizes, *scratch[:6])
@@ -298,28 +301,26 @@
     for p in range(group):
         tails.send[p, :rows] = lost[p * rows : (p + 1) * rows]
         tails.send[p, rows:] = cross[p * less : (p + 1) * less]
+    start(tails.out)
+    for span in spans:
+        for t in range(0, size, 16):
+            for place, term in enumerate(terms(panel_held[t : t + 16, span], 3)):
+                pieces[place * size + t : place * size + t + 16, span] = term
     total, lost_out = sum_pairs(heads.parts())
     heads.column[heads.gz] = total
     start(heads.along)
-    start(tails.out)
-    for span in spans[: steps // 2]:
-        for t, term in enumerate(terms(panel_held[:, span], 3)):
-            pieces[t * size : (t + 1) * size, span] = term
-    total, lost_along = sum_pairs(heads.columns())
-    heads.gathered[heads.me] = total
-    start(heads.back)
     part = sum_plain(tails.parts())
     tails.column[tails.gz, :rows] = part[:rows] + lost_out
     tails.column[tails.gz, rows:] = part[rows:]
     start(tails.along)
-    for span in spans[steps // 2 :]:
-        for t, term in enumerate(terms(panel_held[:, span], 3)):
-            pieces[t * size : (t + 1) * size, span] = term
-    heads.finish()
+    total, lost_along = sum_pairs(heads.columns())
+    heads.gathered[heads.me] = total
+    start(heads.back)
     part = sum_plain(tails.columns())
     tails.gathered[tails.me, :rows] = part[:rows] + lost_along
     tails.gathered[tails.me, rows:] = part[rows:]
     start(tails.back)
+    heads.finish()
     gram = jnp.concatenate([heads.gathered[p] for p in range(group)], axis=0)
     uppers, inverses = factor([gram[h : h + 8] for h in range(0, size, 8)])
     inverse = jnp.concatenate(inverses, axis=0)
@@ -353,15 +354,12 @@
     row = lax.broadcasted_iota(jnp.int32, (size, size), 0)
     lane = lax.broadcasted_iota(jnp.int32, (size, size), 1)
 
-    def correction(value):
-        return jnp.where(row > lane, -value, jnp.where(row == lane, 1.5 - 0.5 * value, 0.0))
-
     moved = product(inverse, off, NN)
     second_gram = product(jnp.concatenate([turned, moved], axis=1), jnp.concatenate([turned, inverse], axis=1), NT)
-    step = correction(second_gram)
-    inverse = product(step, inverse, NN)
-    step = correction(product(product(step, second_gram, NN), step, NT))
-    return product(step, inverse, NN)
+    step = jnp.where(row > lane, second_gram, jnp.where(row == lane, 0.5 * second_gram - 0.5, 0.0))
+    twice = product(step, jnp.concatenate([step, step.T], axis=1), NN)
+    below = jnp.where(row > lane, twice[:, size:], jnp.where(row == lane, 0.5 * twice[:, size:], 0.0))
+    return inverse + product((twice[:, :size] + below) - step, inverse, NN)
 
 
 def final_kernel(scale, gram, rest, off, turned, inverse, pieces, trailing, basis, upper, coupling, updated, basis_held, updated_held, upper_held, coupling_held, store_sem):
@@ -373,11 +371,9 @@
     lost = jnp.concatenate([rest[p, :rows] for p in range(group)], axis=0)
     cross = jnp.concatenate([rest[p, rows:] for p in range(group)], axis=0)
     whole = refine(off[...] + lost, turned[...], inverse[...])
-    left = left_terms(whole * scale)
     mixed = product(cross, whole, NT)
     coupling_held[...] = mixed
-    one, two = terms(mixed * (1.0 / scale), 2)
-    back = jnp.concatenate([two, one, one], axis=1)
+    left = left_terms(jnp.concatenate([whole * scale, product(mixed, whole, NN)], axis=0))
     stores = []
 
     def store(src, dst, place):
@@ -388,10 +384,9 @@
         span, at = slice(i * chunk, (i + 1) * chunk), pl.ds(i * chunk, chunk)
         one, two, three = (pieces[t * size : (t + 1) * size, span] for t in range(3))
         out = dot(left, jnp.concatenate([one, three, two, one, two, one], axis=0), NN)
-        basis_held[:, span] = out
+        basis_held[:, span] = out[:size]
         store(basis_held.at[:, at], basis.at[:, at], 2 * i)
-        one, two = terms(out, 2)
-        updated_held[:, span] = trailing[:, span] - dot(back, jnp.concatenate([one, two, one], axis=0), NN)
+        updated_held[:, span] = trailing[:, span] - out[size:]
         store(updated_held.at[:, at], updated.at[:, at], 2 * i + 1)
         if i == 0:
             row = lax.broadcasted_iota(jnp.int32, (size, size), 0)
@@ -435,7 +430,7 @@
         scratch_shapes=[
             pltpu.VMEM((size, width), f32),
             pltpu.VMEM((3 * size, width), jnp.bfloat16),
-            pltpu.SemaphoreType.DMA((width // chunk_of(width, 512) + 1,)),
+            pltpu.SemaphoreType.DMA((width // chunk_of(width, 1024) + 1,)),
             *exchange_scratch(sizes, rows, size),
             *exchange_scratch(sizes, rows + less, size),
         ],

time: 27.5 us -> 24.9 us (0.905)
  Pallas kernels: 26.7 us -> 24.2 us
    pallas_call x1, Pallas kernels: 22 us -> 20.4 us  [shards(): pl.pallas_call(functools.partial(reduce_kernel, sizes), out_shape=[square...]
    pallas_call x1, Pallas kernels: 4.68 us -> 3.71 us  [shards(): pl.pallas_call(functools.partial(final_kernel, scale), out_shape=[jax.Sha...]
where the time goes in v3:
time: 24.9 us; the launch traced here: 24.8 us
  Pallas kernels  24.2 us (97%)
  between operations  0.64 us (3%)
    pallas_call x1, Pallas kernels, shards(): pl.pallas_call(functools.partial(reduce_kernel, sizes), out_shape=[square...  20.4 us
    pallas_call x1, Pallas kernels, shards(): pl.pallas_call(functools.partial(final_kernel, scale), out_shape=[jax.Sha...  3.71 us

profile of v3, /device:TPU:0, one launch (start us, length us, event | category | flops | bytes accessed | tf_op | source)
XLA Modules:
  0.0 24.8 jit_solution(15203773739364783695)
XLA Ops:
  0.6 20.4 %reduce.1 = (f32[128,128]{1,0:T(8,128)S(1)}, f32[8,24,128]{2,1,0:T(8,128)S(1)}, f32[128,128]{1,0:T(8,128)S(1)}, f32[128,128]{1,0:T(8,128)S(1)}, f32[128,128]{1,0...) custom-call(f32[128,4096]{1,0:T(8,128)} %panel.1, f32[64,4096]{1,0:T(8,128)} %trailing.1), custom_call_target="tpu_custom_call" | custom-call | tf_op jit(solution)/shard_map/reduce/pallas_call | solution.py:417
  21.1 3.7 %final.1 = (f32[128,4096]{1,0:T(8,128)}, f32[128,128]{1,0:T(8,128)}, f32[64,128]{1,0:T(8,128)}, f32[64,4096]{1,0:T(8,128)}) custom-call(f32[128,128]{1,0:T(8,128)S(1)} %get-tuple-element.15.gram, f32[8,24,128]{2,1,0:T(8,128)S(1)} %get-tuple-element.16.rest, f32[128,128]{1,0:T(8,128)S(1)} %get-tuple-element.17.off, f32[128,128]{1,0:T(8,128)S(1)} %get-tuple-element.18.turned, ...), custom_call_target="tpu_custom_call" | custom-call | tf_op jit(solution)/shard_map/final/pallas_call | solution.py:440

commit v4 on v3

--- a/solution.py
+++ b/solution.py
@@ -144,14 +144,24 @@
     return uppers, inverses
 
 
+def plane_peers(sizes, gx, gy):
+    nx, ny, _ = sizes
+    cores = 2 if ny % 2 == 0 else 1
+    chips = ny // cores
+    for dx in range(nx - 1, -1, -1):
+        for dy in range(chips - 1, -1, -1):
+            for core in range(cores):
+                if (dx, dy, core) != (0, 0, 0):
+                    chip = lax.rem(gy // cores + dy, chips)
+                    yield lax.rem(gx + dx, nx), chip * cores + lax.rem(lax.rem(gy, cores) + core, cores)
+
+
 def greet(sizes):
     nx, ny, nz = sizes
     gx, gy, gz = lax.axis_index("gx"), lax.axis_index("gy"), lax.axis_index("gz")
     barrier = pltpu.get_barrier_semaphore()
-    me = gx * ny + gy
-    for step in range(1, nx * ny):
-        peer = lax.rem(me + step, nx * ny)
-        pl.semaphore_signal(barrier, inc=1, device_id=(peer // ny, lax.rem(peer, ny), gz), device_id_type=MESH)
+    for px, py in plane_peers(sizes, gx, gy):
+        pl.semaphore_signal(barrier, inc=1, device_id=(px, py, gz), device_id_type=MESH)
     for step in range(1, nz):
         pl.semaphore_signal(barrier, inc=1, device_id=(gx, gy, lax.rem(gz + step, nz)), device_id_type=MESH)
 
@@ -161,8 +171,8 @@
         nx, ny, nz = sizes
         self.nz, self.group = nz, nx * ny
         self.send, self.landed, self.column, self.gathered = send, landed, column, gathered
+        self.send_sem, self.recv_sem = send_sem, recv_sem
         gx, gy, gz = lax.axis_index("gx"), lax.axis_index("gy"), lax.axis_index("gz")
-        group = self.group
         self.me, self.gz = gx * ny + gy, gz
         me = self.me
 
@@ -171,38 +181,33 @@
                 src_ref=src, dst_ref=dst, send_sem=send_sem.at[at], recv_sem=recv_sem.at[at], device_id=device, device_id_type=MESH
             )
 
-        def in_plane(step):
-            peer = lax.rem(me + step, group)
-            return peer, (peer // ny, lax.rem(peer, ny), gz)
-
         self.out, self.back = [], []
-        for step in range(1, group):
-            peer, device = in_plane(step)
-            self.out.append(copy(send.at[peer], landed.at[step], step, device))
-            self.back.append(copy(gathered.at[me], gathered.at[me], group + nz + step, device))
-        self.along = [
-            copy(column.at[gz], column.at[gz], group + step, (gx, gy, lax.rem(gz + step, nz))) for step in range(1, nz)
-        ]
+        for slot, (px, py) in enumerate(plane_peers(sizes, gx, gy)):
+            self.out.append(copy(send.at[px * ny + py], landed.at[slot], 0, (px, py, gz)))
+            self.back.append(copy(gathered.at[me], gathered.at[me], 2, (px, py, gz)))
+        self.along = [copy(column.at[gz], column.at[gz], 1, (gx, gy, lax.rem(gz + step, nz))) for step in range(nz - 1, 0, -1)]
+
+    def wait(self, ref, sem):
+        pltpu.make_async_copy(ref, ref, sem).wait()
 
     def parts(self):
+        self.wait(self.landed, self.recv_sem.at[0])
         yield self.send[self.me]
-        for step in range(1, self.group):
-            self.out[step - 1].wait_recv()
-            yield self.landed[step]
+        for slot in range(self.group - 1):
+            yield self.landed[slot]
 
     def columns(self):
-        for copy in self.along:
-            copy.wait_recv()
+        self.wait(self.column.at[pl.ds(0, self.nz - 1)], self.recv_sem.at[1])
         for z in range(self.nz):
             yield self.column[z]
 
     def finish(self):
-        for copy in self.back:
-            copy.wait_recv()
+        self.wait(self.gathered.at[pl.ds(0, self.group - 1)], self.recv_sem.at[2])
 
     def drain(self):
-        for copy in self.out + self.along + self.back:
-            copy.wait_send()
+        self.wait(self.landed, self.send_sem.at[0])
+        self.wait(self.column.at[pl.ds(0, self.nz - 1)], self.send_sem.at[1])
+        self.wait(self.gathered.at[pl.ds(0, self.group - 1)], self.send_sem.at[2])
 
 
 def start(copies):
@@ -233,11 +238,11 @@
     group = nx * ny
     return [
         pltpu.VMEM((group, rows, size), jnp.float32),
-        pltpu.VMEM((group, rows, size), jnp.float32),
+        pltpu.VMEM((group - 1, rows, size), jnp.float32),
         pltpu.VMEM((nz, rows, size), jnp.float32),
         pltpu.VMEM((group, rows, size), jnp.float32),
-        pltpu.SemaphoreType.DMA((2 * group + nz,)),
-        pltpu.SemaphoreType.DMA((2 * group + nz,)),
+        pltpu.SemaphoreType.DMA((3,)),
+        pltpu.SemaphoreType.DMA((3,)),
     ]
 
 
@@ -353,13 +358,13 @@
     size = off.shape[0]
     row = lax.broadcasted_iota(jnp.int32, (size, size), 0)
     lane = lax.broadcasted_iota(jnp.int32, (size, size), 1)
-
     moved = product(inverse, off, NN)
     second_gram = product(jnp.concatenate([turned, moved], axis=1), jnp.concatenate([turned, inverse], axis=1), NT)
     step = jnp.where(row > lane, second_gram, jnp.where(row == lane, 0.5 * second_gram - 0.5, 0.0))
-    twice = product(step, jnp.concatenate([step, step.T], axis=1), NN)
-    below = jnp.where(row > lane, twice[:, size:], jnp.where(row == lane, 0.5 * twice[:, size:], 0.0))
-    return inverse + product((twice[:, :size] + below) - step, inverse, NN)
+    narrow = step.astype(jnp.bfloat16)
+    square = dot(narrow, narrow, NN)
+    twice = dot(narrow, narrow, NT)
+    return (square + jnp.where(row > lane, twice, jnp.where(row == lane, 0.5 * twice, 0.0))) - step
 
 
 def final_kernel(scale, gram, rest, off, turned, inverse, pieces, trailing, basis, upper, coupling, updated, basis_held, updated_held, upper_held, coupling_held, store_sem):
@@ -370,10 +375,13 @@
     rows = size // group
     lost = jnp.concatenate([rest[p, :rows] for p in range(group)], axis=0)
     cross = jnp.concatenate([rest[p, rows:] for p in range(group)], axis=0)
-    whole = refine(off[...] + lost, turned[...], inverse[...])
-    mixed = product(cross, whole, NT)
+    inverse = inverse[...]
+    mixed = product(cross, inverse, NT)
+    change = refine(off[...] + lost, turned[...], inverse)
+    whole = inverse + product(change, inverse, NN)
+    mixed = mixed + product(mixed, change, NT)
     coupling_held[...] = mixed
-    left = left_terms(jnp.concatenate([whole * scale, product(mixed, whole, NN)], axis=0))
+    left = left_terms(whole * scale)
     stores = []
 
     def store(src, dst, place):
@@ -383,10 +391,17 @@
     for i in range(steps):
         span, at = slice(i * chunk, (i + 1) * chunk), pl.ds(i * chunk, chunk)
         one, two, three = (pieces[t * size : (t + 1) * size, span] for t in range(3))
-        out = dot(left, jnp.concatenate([one, three, two, one, two, one], axis=0), NN)
+        right = jnp.concatenate([one, three, two, one, two, one], axis=0)
+        out = dot(left, right, NN)
         basis_held[:, span] = out[:size]
         store(basis_held.at[:, at], basis.at[:, at], 2 * i)
-        updated_held[:, span] = trailing[:, span] - out[size:]
+        if i == 0:
+            more = left_terms(product(mixed, whole, NN))
+            left = jnp.concatenate([left, more], axis=0)
+            projected = dot(more, right, NN)
+        else:
+            projected = out[size:]
+        updated_held[:, span] = trailing[:, span] - projected
         store(updated_held.at[:, at], updated.at[:, at], 2 * i + 1)
         if i == 0:
             row = lax.broadcasted_iota(jnp.int32, (size, size), 0)

time: 24.9 us -> 23.9 us (0.960)
  Pallas kernels: 24.2 us -> 23.1 us
    pallas_call x1, Pallas kernels: 20.4 us -> 19.6 us  [shards(): pl.pallas_call(functools.partial(reduce_kernel, sizes), out_shape=[square...]
where the time goes in v4:
time: 23.9 us; the launch traced here: 23.8 us
  Pallas kernels  23.1 us (97%)
  between operations  0.64 us (3%)
    pallas_call x1, Pallas kernels, shards(): pl.pallas_call(functools.partial(reduce_kernel, sizes), out_shape=[square...  19.6 us
    pallas_call x1, Pallas kernels, shards(): pl.pallas_call(functools.partial(final_kernel, scale), out_shape=[jax.Sha...  3.48 us

profile of v4, /device:TPU:0, one launch (start us, length us, event | category | flops | bytes accessed | tf_op | source)
XLA Modules:
  0.0 23.8 jit_solution(14294151637251800237)
XLA Ops:
  0.6 19.6 %reduce.1 = (f32[128,128]{1,0:T(8,128)S(1)}, f32[8,24,128]{2,1,0:T(8,128)S(1)}, f32[128,128]{1,0:T(8,128)S(1)}, f32[128,128]{1,0:T(8,128)S(1)}, f32[128,128]{1,0...) custom-call(f32[128,4096]{1,0:T(8,128)} %panel.1, f32[64,4096]{1,0:T(8,128)} %trailing.1), custom_call_target="tpu_custom_call" | custom-call | tf_op jit(solution)/shard_map/reduce/pallas_call | solution.py:432
  20.3 3.5 %final.1 = (f32[128,4096]{1,0:T(8,128)}, f32[128,128]{1,0:T(8,128)}, f32[64,128]{1,0:T(8,128)}, f32[64,4096]{1,0:T(8,128)}) custom-call(f32[128,128]{1,0:T(8,128)S(1)} %get-tuple-element.15.gram, f32[8,24,128]{2,1,0:T(8,128)S(1)} %get-tuple-element.16.rest, f32[128,128]{1,0:T(8,128)S(1)} %get-tuple-element.17.off, f32[128,128]{1,0:T(8,128)S(1)} %get-tuple-element.18.turned, ...), custom_call_target="tpu_custom_call" | custom-call | tf_op jit(solution)/shard_map/final/pallas_call | solution.py:455

commit v5 on v4

--- a/solution.py
+++ b/solution.py
@@ -47,8 +47,11 @@
     high = (value + top) - top
     rest = value - high
     top = top * 2.0**-9
-    middle = (rest + top) - top
-    return high.astype(jnp.bfloat16), middle.astype(jnp.bfloat16), (rest - middle).astype(jnp.bfloat16)
+    return high, (rest + top) - top
+
+
+def narrow(*values):
+    return jnp.concatenate([value.astype(jnp.bfloat16) for value in values], axis=0)
 
 
 def two_sum(one, two):
@@ -255,13 +258,14 @@
     return most if width % most == 0 else width
 
 
-def reduce_kernel(sizes, panel, trailing, gram_out, rest_out, off_out, product_out, inverse_out, pieces, trailing_held, panel_held, sliced, move_sem, *scratch):
+def reduce_kernel(sizes, panel, trailing, gram_out, rest_out, off_out, product_out, inverse_out, pieces, trailing_held, panel_held, move_sem, *scratch):
     size, width = panel.shape
     trail = trailing.shape[0]
     group = sizes[0] * sizes[1]
     rows, less = size // group, trail // group
     chunk = chunk_of(width, 1024)
     steps = width // chunk
+    sliced = scratch[12:]
     spans = [slice(i * chunk, (i + 1) * chunk) for i in range(steps)]
     loads = []
     for i in range(steps):
@@ -270,39 +274,47 @@
     loads.append(pltpu.make_async_copy(trailing, trailing_held, move_sem.at[steps]))
     start(loads)
     greet(sizes)
+    none = lax.axis_index("gx") // sizes[0]
     zero = jnp.zeros((size, size), jnp.float32)
-    gram, lost, mixed, small = zero, zero, zero, zero
+    gram, lost, small = zero, zero, zero
     for i in range(steps + 1):
         if i < steps:
             loads[i].wait()
             for t in range(0, size, 16):
                 for place, part in enumerate(slices(panel_held[t : t + 16, spans[i]])):
-                    sliced[place * size + t : place * size + t + 16, spans[i]] = part
+                    sliced[i][0, place * size + t : place * size + t + 16] = part.astype(jnp.bfloat16)
         if i > 0:
-            for half in halves(spans[i - 1]):
-                found = dot(sliced[:, half], sliced[: 2 * size, half], NT)
+            for half in halves(slice(0, chunk)):
+                pair = sliced[i - 1][none, :, half]
+                found = dot(pair, pair, NT)
                 gram, off = two_sum(gram, found[:size, :size])
                 lost = lost + off
-                mixed = mixed + (found[:size, size:] + (found[2 * size :, :size] + found[2 * size :, size:]))
-                small = small + found[size : 2 * size, size:]
-    gram, off = two_sum(gram, small + (mixed + mixed.T))
+                small = small + ((found[:size, size:] + found[size:, :size]) + found[size:, size:])
+    gram, off = two_sum(gram, small)
     lost = lost + off
     heads = Exchange(sizes, *scratch[:6])
-    tails = Exchange(sizes, *scratch[6:])
+    tails = Exchange(sizes, *scratch[6:12])
     for p in range(group):
         heads.send[p] = gram[p * rows : (p + 1) * rows]
     pl.semaphore_wait(pltpu.get_barrier_semaphore(), group - 1 + sizes[2] - 1)
     start(heads.out)
     loads[steps].wait()
     cross = jnp.zeros((trail, size), jnp.float32)
-    for span in spans:
-        both = jnp.concatenate(terms(trailing_held[:, span], 2), axis=0)
-        low = sliced[2 * size :, span]
-        found = dot(both, sliced[: 2 * size, span], NT)
-        last = dot(jnp.concatenate([low, both], axis=0), low, NT)
-        found = found[:, :size] + (found[:, size:] + last[size:])
+    lows = zero
+    for i, span in enumerate(spans):
+        pair = sliced[i][none]
+        low = (panel_held[:, span] - pair[:size].astype(jnp.float32)) - pair[size:].astype(jnp.float32)
+        low = low.astype(jnp.bfloat16)
+        one, two = terms(trailing_held[:, span], 2)
+        left = jnp.concatenate([low, one, two], axis=0)
+        found = dot(left, pair, NT)
+        last = dot(left, low, NT)
+        found = found[:, :size] + found[:, size:]
+        lows = lows + found[:size]
+        lost = lost + last[:size]
+        found = found[size:] + last[size:]
         cross = cross + (found[:trail] + found[trail:])
-        lost = lost + last[:size]
+    lost = lost + (lows + lows.T)
     for p in range(group):
         tails.send[p, :rows] = lost[p * rows : (p + 1) * rows]
         tails.send[p, rows:] = cross[p * less : (p + 1) * less]
@@ -343,14 +355,16 @@
 
 def departure(gram, upper, inverse):
     size = gram.shape[0]
-    high, middle, low = slices(upper.T)
-    pair = jnp.concatenate([high, middle], axis=0)
+    lower = upper.T
+    high, middle = slices(lower)
+    low = ((lower - high) - middle).astype(jnp.bfloat16)
+    pair = narrow(high, middle)
     first = dot(pair, pair, NT)
     second = dot(low, pair, NT)
     mixed = first[:size, size:] + (second[:, :size] + second[:, size:])
     small = (first[size:, size:] + dot(low, low, NT)) + (mixed + mixed.T)
     off, lower_off = two_sum(gram, -first[:size, :size])
-    lower = (high.astype(jnp.float32) + middle.astype(jnp.float32)) + low.astype(jnp.float32)
+    lower = (high + middle) + low.astype(jnp.float32)
     return (off - small) + lower_off, product(inverse, lower, NN)
 
 
@@ -361,9 +375,9 @@
     moved = product(inverse, off, NN)
     second_gram = product(jnp.concatenate([turned, moved], axis=1), jnp.concatenate([turned, inverse], axis=1), NT)
     step = jnp.where(row > lane, second_gram, jnp.where(row == lane, 0.5 * second_gram - 0.5, 0.0))
-    narrow = step.astype(jnp.bfloat16)
-    square = dot(narrow, narrow, NN)
-    twice = dot(narrow, narrow, NT)
+    rough = step.astype(jnp.bfloat16)
+    square = dot(rough, rough, NN)
+    twice = dot(rough, rough, NT)
     return (square + jnp.where(row > lane, twice, jnp.where(row == lane, 0.5 * twice, 0.0))) - step
 
 
@@ -444,10 +458,10 @@
         out_specs=[VMEM] * 7,
         scratch_shapes=[
             pltpu.VMEM((size, width), f32),
-            pltpu.VMEM((3 * size, width), jnp.bfloat16),
             pltpu.SemaphoreType.DMA((width // chunk_of(width, 1024) + 1,)),
             *exchange_scratch(sizes, rows, size),
             *exchange_scratch(sizes, rows + less, size),
+            *[pltpu.VMEM((1, 2 * size, chunk_of(width, 1024)), jnp.bfloat16) for _ in range(width // chunk_of(width, 1024))],
         ],
         compiler_params=params(0),
         name="reduce",

time: 23.9 us -> 23.5 us (0.983)
  Pallas kernels: 23.1 us -> 22.8 us
    pallas_call x1, Pallas kernels: 19.6 us -> 19.3 us  [shards(): pl.pallas_call(functools.partial(reduce_kernel, sizes), out_shape=[square...]
where the time goes in v5:
time: 23.5 us; the launch traced here: 23.4 us
  Pallas kernels  22.8 us (97%)
  between operations  0.64 us (3%)
    pallas_call x1, Pallas kernels, shards(): pl.pallas_call(functools.partial(reduce_kernel, sizes), out_shape=[square...  19.3 us
    pallas_call x1, Pallas kernels, shards(): pl.pallas_call(functools.partial(final_kernel, scale), out_shape=[jax.Sha...  3.48 us

profile of v5, /device:TPU:0, one launch (start us, length us, event | category | flops | bytes accessed | tf_op | source)
XLA Modules:
  0.0 23.4 jit_solution(488561477851242143)
XLA Ops:
  0.6 19.3 %reduce.1 = (f32[128,128]{1,0:T(8,128)S(1)}, f32[8,24,128]{2,1,0:T(8,128)S(1)}, f32[128,128]{1,0:T(8,128)S(1)}, f32[128,128]{1,0:T(8,128)S(1)}, f32[128,128]{1,0...) custom-call(f32[128,4096]{1,0:T(8,128)} %panel.1, f32[64,4096]{1,0:T(8,128)} %trailing.1), custom_call_target="tpu_custom_call" | custom-call | tf_op jit(solution)/shard_map/reduce/pallas_call | solution.py:446
  19.9 3.5 %final.1 = (f32[128,4096]{1,0:T(8,128)}, f32[128,128]{1,0:T(8,128)}, f32[64,128]{1,0:T(8,128)}, f32[64,4096]{1,0:T(8,128)}) custom-call(f32[128,128]{1,0:T(8,128)S(1)} %get-tuple-element.15.gram, f32[8,24,128]{2,1,0:T(8,128)S(1)} %get-tuple-element.16.rest, f32[128,128]{1,0:T(8,128)S(1)} %get-tuple-element.17.off, f32[128,128]{1,0:T(8,128)S(1)} %get-tuple-element.18.turned, ...), custom_call_target="tpu_custom_call" | custom-call | tf_op jit(solution)/shard_map/final/pallas_call | solution.py:469

commit v6 on v5

--- a/solution.py
+++ b/solution.py
@@ -258,18 +258,22 @@
     return most if width % most == 0 else width
 
 
-def reduce_kernel(sizes, panel, trailing, gram_out, rest_out, off_out, product_out, inverse_out, pieces, trailing_held, panel_held, move_sem, *scratch):
+def spans_of(width):
+    chunk = chunk_of(width, 1024)
+    return [slice(at, at + chunk) for at in range(0, width, chunk)]
+
+
+def reduce_kernel(sizes, panel, trailing, gram_out, rest_out, upper_out, inverse_out, pieces, trailing_held, panel_held, move_sem, *scratch):
     size, width = panel.shape
     trail = trailing.shape[0]
     group = sizes[0] * sizes[1]
     rows, less = size // group, trail // group
-    chunk = chunk_of(width, 1024)
-    steps = width // chunk
+    spans = spans_of(width)
+    steps = len(spans)
     sliced = scratch[12:]
-    spans = [slice(i * chunk, (i + 1) * chunk) for i in range(steps)]
     loads = []
-    for i in range(steps):
-        at = pl.ds(i * chunk, chunk)
+    for i, span in enumerate(spans):
+        at = pl.ds(span.start, span.stop - span.start)
         loads.append(pltpu.make_async_copy(panel.at[:, at], panel_held.at[:, at], move_sem.at[i]))
     loads.append(pltpu.make_async_copy(trailing, trailing_held, move_sem.at[steps]))
     start(loads)
@@ -284,7 +288,7 @@
                 for place, part in enumerate(slices(panel_held[t : t + 16, spans[i]])):
                     sliced[i][0, place * size + t : place * size + t + 16] = part.astype(jnp.bfloat16)
         if i > 0:
-            for half in halves(slice(0, chunk)):
+            for half in halves(slice(0, spans[i - 1].stop - spans[i - 1].start)):
                 pair = sliced[i - 1][none, :, half]
                 found = dot(pair, pair, NT)
                 gram, off = two_sum(gram, found[:size, :size])
@@ -340,12 +344,9 @@
     heads.finish()
     gram = jnp.concatenate([heads.gathered[p] for p in range(group)], axis=0)
     uppers, inverses = factor([gram[h : h + 8] for h in range(0, size, 8)])
-    inverse = jnp.concatenate(inverses, axis=0)
     gram_out[...] = gram
-    inverse_out[...] = inverse
-    off, turned = departure(gram, jnp.concatenate(uppers, axis=0), inverse)
-    off_out[...] = off
-    product_out[...] = turned
+    upper_out[...] = jnp.concatenate(uppers, axis=0)
+    inverse_out[...] = jnp.concatenate(inverses, axis=0)
     tails.finish()
     for p in range(group):
         rest_out[p] = tails.gathered[p]
@@ -381,7 +382,7 @@
     return (square + jnp.where(row > lane, twice, jnp.where(row == lane, 0.5 * twice, 0.0))) - step
 
 
-def final_kernel(scale, gram, rest, off, turned, inverse, pieces, trailing, basis, upper, coupling, updated, basis_held, updated_held, upper_held, coupling_held, store_sem):
+def final_kernel(scale, gram, rest, first_upper, inverse, pieces, trailing, basis, upper, coupling, updated, basis_held, updated_held, upper_held, coupling_held, both_held, store_sem):
     size, width = basis.shape
     chunk = chunk_of(width, 512)
     steps = width // chunk
@@ -389,13 +390,32 @@
     rows = size // group
     lost = jnp.concatenate([rest[p, :rows] for p in range(group)], axis=0)
     cross = jnp.concatenate([rest[p, rows:] for p in range(group)], axis=0)
-    inverse = inverse[...]
+    gram, inverse = gram[...], inverse[...]
+    off, turned = departure(gram, first_upper[...], inverse)
     mixed = product(cross, inverse, NT)
-    change = refine(off[...] + lost, turned[...], inverse)
-    whole = inverse + product(change, inverse, NN)
+    left = left_terms(inverse * scale)
+    for i in range(steps):
+        span = slice(i * chunk, (i + 1) * chunk)
+        one, two, three = (pieces[t * size : (t + 1) * size, span] for t in range(3))
+        first = dot(left, jnp.concatenate([one, three, two, one, two, one], axis=0), NN)
+        basis_held[:, span] = first
+        one, two = terms(first, 2)
+        both_held[:size, span] = one
+        both_held[size:, span] = two
+    change = refine(off + lost, turned, inverse)
     mixed = mixed + product(mixed, change, NT)
     coupling_held[...] = mixed
-    left = left_terms(whole * scale)
+    back = (mixed + product(mixed, change, NN)) * (1.0 / scale)
+    one, two = terms(back, 2)
+    rough = change.astype(jnp.bfloat16)
+    left = jnp.concatenate(
+        [
+            jnp.concatenate([rough, rough], axis=1),
+            jnp.concatenate([one, one], axis=1),
+            jnp.concatenate([two, jnp.zeros_like(two)], axis=1),
+        ],
+        axis=0,
+    )
     stores = []
 
     def store(src, dst, place):
@@ -404,23 +424,16 @@
 
     for i in range(steps):
         span, at = slice(i * chunk, (i + 1) * chunk), pl.ds(i * chunk, chunk)
-        one, two, three = (pieces[t * size : (t + 1) * size, span] for t in range(3))
-        right = jnp.concatenate([one, three, two, one, two, one], axis=0)
-        out = dot(left, right, NN)
-        basis_held[:, span] = out[:size]
+        out = dot(left, both_held[:, span], NN)
+        basis_held[:, span] = basis_held[:, span] + out[:size]
         store(basis_held.at[:, at], basis.at[:, at], 2 * i)
-        if i == 0:
-            more = left_terms(product(mixed, whole, NN))
-            left = jnp.concatenate([left, more], axis=0)
-            projected = dot(more, right, NN)
-        else:
-            projected = out[size:]
-        updated_held[:, span] = trailing[:, span] - projected
+        updated_held[:, span] = trailing[:, span] - (out[size : size + back.shape[0]] + out[size + back.shape[0] :])
         store(updated_held.at[:, at], updated.at[:, at], 2 * i + 1)
         if i == 0:
             row = lax.broadcasted_iota(jnp.int32, (size, size), 0)
             lane = lax.broadcasted_iota(jnp.int32, (size, size), 1)
-            total = product(whole, gram[...], NN) + product(whole, lost, NN)
+            whole = inverse + product(change, inverse, NN)
+            total = product(whole, gram, NN) + product(whole, lost, NN)
             upper_held[...] = jnp.where(row <= lane, total * (1.0 / scale), 0.0)
             store(coupling_held, coupling, 2 * steps)
             store(upper_held, upper, 2 * steps + 1)
@@ -450,18 +463,17 @@
             jax.ShapeDtypeStruct((group, rows + less, size), f32),
             square,
             square,
-            square,
             jax.ShapeDtypeStruct((3 * size, width), jnp.bfloat16),
             jax.ShapeDtypeStruct((trail, width), f32),
         ],
         in_specs=[HBM, HBM],
-        out_specs=[VMEM] * 7,
+        out_specs=[VMEM] * 6,
         scratch_shapes=[
             pltpu.VMEM((size, width), f32),
-            pltpu.SemaphoreType.DMA((width // chunk_of(width, 1024) + 1,)),
+            pltpu.SemaphoreType.DMA((len(spans_of(width)) + 1,)),
             *exchange_scratch(sizes, rows, size),
             *exchange_scratch(sizes, rows + less, size),
-            *[pltpu.VMEM((1, 2 * size, chunk_of(width, 1024)), jnp.bfloat16) for _ in range(width // chunk_of(width, 1024))],
+            *[pltpu.VMEM((1, 2 * size, span.stop - span.start), jnp.bfloat16) for span in spans_of(width)],
         ],
         compiler_params=params(0),
         name="reduce",
@@ -474,13 +486,14 @@
             jax.ShapeDtypeStruct((trail, size), f32),
             jax.ShapeDtypeStruct((trail, width), f32),
         ],
-        in_specs=[VMEM] * 7,
+        in_specs=[VMEM] * 6,
         out_specs=[HBM] * 4,
         scratch_shapes=[
             pltpu.VMEM((size, width), f32),
             pltpu.VMEM((trail, width), f32),
             pltpu.VMEM((size, size), f32),
             pltpu.VMEM((trail, size), f32),
+            pltpu.VMEM((2 * size, width), jnp.bfloat16),
             pltpu.SemaphoreType.DMA((2 * (width // chunk_of(width, 512)) + 2,)),
         ],
         compiler_params=params(),

time: 23.5 us -> 24.1 us (1.026)
  Pallas kernels: 22.8 us -> 23.3 us
    pallas_call x1, Pallas kernels: 3.48 us -> 4.4 us  [shards(): pl.pallas_call(functools.partial(final_kernel, scale), out_shape=[jax.Sha...]
    pallas_call x1, Pallas kernels: 19.3 us -> 18.9 us  [shards(): pl.pallas_call(functools.partial(reduce_kernel, sizes), out_shape=[square...]
where the time goes in v6:
time: 24.1 us; the launch traced here: 23.9 us
  Pallas kernels  23.3 us (97%)
  between operations  0.64 us (3%)
    pallas_call x1, Pallas kernels, shards(): pl.pallas_call(functools.partial(reduce_kernel, sizes), out_shape=[square...  18.9 us
    pallas_call x1, Pallas kernels, shards(): pl.pallas_call(functools.partial(final_kernel, scale), out_shape=[jax.Sha...  4.4 us

profile of v6, /device:TPU:0, one launch (start us, length us, event | category | flops | bytes accessed | tf_op | source)
XLA Modules:
  0.0 23.9 jit_solution(14392735610511036099)
XLA Ops:
  0.6 18.9 %reduce.1 = (f32[128,128]{1,0:T(8,128)S(1)}, f32[8,24,128]{2,1,0:T(8,128)S(1)}, f32[128,128]{1,0:T(8,128)S(1)}, f32[128,128]{1,0:T(8,128)S(1)}, bf16[384,4096]{1,0:T(8,128)(2,1)S(1)}, /*index=5*/f32[64,4096]{1,0:T(8,128)S(1)}) custom-call(f32[128,4096]{1,0:T(8,128)} %panel.1, f32[64,4096]{1,0:T(8,128)} %trailing.1), custom_call_target="tpu_custom_call" | custom-call | tf_op jit(solution)/shard_map/reduce/pallas_call | solution.py:459
  19.5 4.4 %final.1 = (f32[128,4096]{1,0:T(8,128)}, f32[128,128]{1,0:T(8,128)}, f32[64,128]{1,0:T(8,128)}, f32[64,4096]{1,0:T(8,128)}) custom-call(f32[128,128]{1,0:T(8,128)S(1)} %get-tuple-element.14.gram, f32[8,24,128]{2,1,0:T(8,128)S(1)} %get-tuple-element.15.rest, f32[128,128]{1,0:T(8,128)S(1)} %get-tuple-element.16.first_upper, ...), custom_call_target="tpu_custom_call" | custom-call | tf_op jit(solution)/shard_map/final/pallas_call | solution.py:481

commit v7 on v5

--- a/solution.py
+++ b/solution.py
@@ -42,6 +42,13 @@
     return dot(left_terms(left), right_terms(right, 1 if dims is NT else 0), dims)
 
 
+def close_product(left, right, dims):
+    one, two = terms(left, 2)
+    first, second = terms(right, 2)
+    axis = 1 if dims is NT else 0
+    return dot(jnp.concatenate([two, one, one], axis=1), jnp.concatenate([first, second, first], axis=axis), dims)
+
+
 def slices(value):
     top = jnp.max(jnp.abs(value), axis=1, keepdims=True) * 2.0**17
     high = (value + top) - top
@@ -67,6 +74,7 @@
     row_in_tile = lax.broadcasted_iota(jnp.int32, shape, 0)
     tiles = list(tiles)
     count = len(tiles)
+    every = []
 
     def across(tile, column):
         return jnp.broadcast_to(jnp.sum(jnp.where(lanes == column, tile, 0.0), axis=1, keepdims=True), shape)
@@ -113,6 +121,7 @@
                         after[j] = after[j] - times * down(column, j)
             tiles[at] = tile
             scales.append(scale)
+            every.append(scale)
             for h in range(at + 2, stop):
                 columns = [across(raw[h], first + j) for j in range(8)]
                 total = tiles[h]
@@ -132,17 +141,15 @@
                 right.append(jnp.where(lanes == rows, 1.0, jnp.where(inner & (lanes > rows), 0.0, tiles[h])) * scales[h - start])
             b1, b2, b3 = terms(jnp.concatenate(right, axis=0), 3)
             a1, a2, a3 = terms(left, 3)
-            a = jnp.concatenate([a3, a1, a2, a2, a1, a1], axis=0)
-            update = dot(a, jnp.concatenate([b1, b3, b2, b1, b2, b1], axis=0), TN)
+            update = dot(jnp.concatenate([a3, a1, a2], axis=0), jnp.concatenate([b1, b3, b2], axis=0), TN)
+            update = update + dot(jnp.concatenate([a2, a1, a1], axis=0), jnp.concatenate([b1, b2, b1], axis=0), TN)
             for h in range(stop, count):
                 tiles[h] = jnp.where(inner, 0.0, tiles[h]) - update[8 * h : 8 * h + 8]
     uppers, inverses = [], []
     for h, tile in enumerate(tiles):
         rows = row_in_tile + 8 * h
-        pivot = jnp.sum(jnp.where(lanes == rows, tile, 0.0), axis=1, keepdims=True)
-        root = jnp.sqrt(pivot)
-        over = 1.0 / root
-        uppers.append(jnp.where(lanes > rows, tile * over, jnp.where(lanes == rows, root, 0.0)))
+        over = jnp.sqrt(every[h])
+        uppers.append(jnp.where(lanes > rows, tile * over, jnp.where(lanes == rows, 1.0 / over, 0.0)))
         inverses.append(jnp.where(lanes < rows, tile * over, jnp.where(lanes == rows, over, 0.0)))
     return uppers, inverses
 
@@ -372,8 +379,8 @@
     size = off.shape[0]
     row = lax.broadcasted_iota(jnp.int32, (size, size), 0)
     lane = lax.broadcasted_iota(jnp.int32, (size, size), 1)
-    moved = product(inverse, off, NN)
-    second_gram = product(jnp.concatenate([turned, moved], axis=1), jnp.concatenate([turned, inverse], axis=1), NT)
+    moved = close_product(inverse, off, NN)
+    second_gram = close_product(turned, turned, NT) + close_product(moved, inverse, NT)
     step = jnp.where(row > lane, second_gram, jnp.where(row == lane, 0.5 * second_gram - 0.5, 0.0))
     rough = step.astype(jnp.bfloat16)
     square = dot(rough, rough, NN)
@@ -393,9 +400,9 @@
     mixed = product(cross, inverse, NT)
     change = refine(off[...] + lost, turned[...], inverse)
     whole = inverse + product(change, inverse, NN)
-    mixed = mixed + product(mixed, change, NT)
+    mixed = mixed + close_product(mixed, change, NT)
     coupling_held[...] = mixed
-    left = left_terms(whole * scale)
+    left = left_terms(jnp.concatenate([whole * scale, product(mixed, whole, NN)], axis=0))
     stores = []
 
     def store(src, dst, place):
@@ -409,18 +416,13 @@
         out = dot(left, right, NN)
         basis_held[:, span] = out[:size]
         store(basis_held.at[:, at], basis.at[:, at], 2 * i)
-        if i == 0:
-            more = left_terms(product(mixed, whole, NN))
-            left = jnp.concatenate([left, more], axis=0)
-            projected = dot(more, right, NN)
-        else:
-            projected = out[size:]
+        projected = out[size:]
         updated_held[:, span] = trailing[:, span] - projected
         store(updated_held.at[:, at], updated.at[:, at], 2 * i + 1)
-        if i == 0:
+        if i == steps - 1:
             row = lax.broadcasted_iota(jnp.int32, (size, size), 0)
             lane = lax.broadcasted_iota(jnp.int32, (size, size), 1)
-            total = product(whole, gram[...], NN) + product(whole, lost, NN)
+            total = product(whole, gram[...], NN) + dot(whole.astype(jnp.bfloat16), lost.astype(jnp.bfloat16), NN)
             upper_held[...] = jnp.where(row <= lane, total * (1.0 / scale), 0.0)
             store(coupling_held, coupling, 2 * steps)
             store(upper_held, upper, 2 * steps + 1)

time: 23.5 us -> 23.2 us (0.987)
  Pallas kernels: 22.8 us -> 22.4 us
    pallas_call x1, Pallas kernels: 3.48 us -> 3.15 us  [shards(): pl.pallas_call(functools.partial(final_kernel, scale), out_shape=[jax.Sha...]
where the time goes in v7:
time: 23.2 us; the launch traced here: 23 us
  Pallas kernels  22.4 us (97%)
  between operations  0.64 us (3%)
    pallas_call x1, Pallas kernels, shards(): pl.pallas_call(functools.partial(reduce_kernel, sizes), out_shape=[square...  19.2 us
    pallas_call x1, Pallas kernels, shards(): pl.pallas_call(functools.partial(final_kernel, scale), out_shape=[jax.Sha...  3.15 us

profile of v7, /device:TPU:0, one launch (start us, length us, event | category | flops | bytes accessed | tf_op | source)
XLA Modules:
  0.0 23.0 jit_solution(14287898877508130316)
XLA Ops:
  0.6 19.2 %reduce.1 = (f32[128,128]{1,0:T(8,128)S(1)}, f32[8,24,128]{2,1,0:T(8,128)S(1)}, f32[128,128]{1,0:T(8,128)S(1)}, f32[128,128]{1,0:T(8,128)S(1)}, f32[128,128]{1,0...) custom-call(f32[128,4096]{1,0:T(8,128)} %panel.1, f32[64,4096]{1,0:T(8,128)} %trailing.1), custom_call_target="tpu_custom_call" | custom-call | tf_op jit(solution)/shard_map/reduce/pallas_call | solution.py:448
  19.9 3.1 %final.1 = (f32[128,4096]{1,0:T(8,128)}, f32[128,128]{1,0:T(8,128)}, f32[64,128]{1,0:T(8,128)}, f32[64,4096]{1,0:T(8,128)}) custom-call(f32[128,128]{1,0:T(8,128)S(1)} %get-tuple-element.15.gram, f32[8,24,128]{2,1,0:T(8,128)S(1)} %get-tuple-element.16.rest, f32[128,128]{1,0:T(8,128)S(1)} %get-tuple-element.17.off, f32[128,128]{1,0:T(8,128)S(1)} %get-tuple-element.18.turned, ...), custom_call_target="tpu_custom_call" | custom-call | tf_op jit(solution)/shard_map/final/pallas_call | solution.py:471

commit v8 on v7

--- a/solution.py
+++ b/solution.py
@@ -325,11 +325,11 @@
     for p in range(group):
         tails.send[p, :rows] = lost[p * rows : (p + 1) * rows]
         tails.send[p, rows:] = cross[p * less : (p + 1) * less]
-    start(tails.out)
     for span in spans:
         for t in range(0, size, 16):
             for place, term in enumerate(terms(panel_held[t : t + 16, span], 3)):
                 pieces[place * size + t : place * size + t + 16, span] = term
+    start(tails.out)
     total, lost_out = sum_pairs(heads.parts())
     heads.column[heads.gz] = total
     start(heads.along)

time: 23.2 us -> 23.1 us (level)
  no operation moved by 1% of the time
where the time goes in v8:
time: 23.1 us; the launch traced here: 22.9 us
  Pallas kernels  22.3 us (97%)
  between operations  0.64 us (3%)
    pallas_call x1, Pallas kernels, shards(): pl.pallas_call(functools.partial(reduce_kernel, sizes), out_shape=[square...  19.1 us
    pallas_call x1, Pallas kernels, shards(): pl.pallas_call(functools.partial(final_kernel, scale), out_shape=[jax.Sha...  3.15 us

profile of v8, /device:TPU:0, one launch (start us, length us, event | category | flops | bytes accessed | tf_op | source)
XLA Modules:
  0.0 22.9 jit_solution(13777863067838488406)
XLA Ops:
  0.6 19.1 %reduce.1 = (f32[128,128]{1,0:T(8,128)S(1)}, f32[8,24,128]{2,1,0:T(8,128)S(1)}, f32[128,128]{1,0:T(8,128)S(1)}, f32[128,128]{1,0:T(8,128)S(1)}, f32[128,128]{1,0...) custom-call(f32[128,4096]{1,0:T(8,128)} %panel.1, f32[64,4096]{1,0:T(8,128)} %trailing.1), custom_call_target="tpu_custom_call" | custom-call | tf_op jit(solution)/shard_map/reduce/pallas_call | solution.py:448
  19.8 3.1 %final.1 = (f32[128,4096]{1,0:T(8,128)}, f32[128,128]{1,0:T(8,128)}, f32[64,128]{1,0:T(8,128)}, f32[64,4096]{1,0:T(8,128)}) custom-call(f32[128,128]{1,0:T(8,128)S(1)} %get-tuple-element.15.gram, f32[8,24,128]{2,1,0:T(8,128)S(1)} %get-tuple-element.16.rest, f32[128,128]{1,0:T(8,128)S(1)} %get-tuple-element.17.off, f32[128,128]{1,0:T(8,128)S(1)} %get-tuple-element.18.turned, ...), custom_call_target="tpu_custom_call" | custom-call | tf_op jit(solution)/shard_map/final/pallas_call | solution.py:471

commit v9 on v8

--- a/solution.py
+++ b/solution.py
@@ -265,18 +265,25 @@
     return most if width % most == 0 else width
 
 
+def spans_of(width):
+    wide, thin = 1024, 512
+    if width % wide:
+        return [slice(0, width)]
+    edges = [0, thin, *range(wide, width + 1, wide)]
+    return [slice(low, high) for low, high in zip(edges[:-1], edges[1:])]
+
+
 def reduce_kernel(sizes, panel, trailing, gram_out, rest_out, off_out, product_out, inverse_out, pieces, trailing_held, panel_held, move_sem, *scratch):
     size, width = panel.shape
     trail = trailing.shape[0]
     group = sizes[0] * sizes[1]
     rows, less = size // group, trail // group
-    chunk = chunk_of(width, 1024)
-    steps = width // chunk
+    spans = spans_of(width)
+    steps = len(spans)
     sliced = scratch[12:]
-    spans = [slice(i * chunk, (i + 1) * chunk) for i in range(steps)]
     loads = []
-    for i in range(steps):
-        at = pl.ds(i * chunk, chunk)
+    for i, span in enumerate(spans):
+        at = pl.ds(span.start, span.stop - span.start)
         loads.append(pltpu.make_async_copy(panel.at[:, at], panel_held.at[:, at], move_sem.at[i]))
     loads.append(pltpu.make_async_copy(trailing, trailing_held, move_sem.at[steps]))
     start(loads)
@@ -291,7 +298,7 @@
                 for place, part in enumerate(slices(panel_held[t : t + 16, spans[i]])):
                     sliced[i][0, place * size + t : place * size + t + 16] = part.astype(jnp.bfloat16)
         if i > 0:
-            for half in halves(slice(0, chunk)):
+            for half in halves(slice(0, spans[i - 1].stop - spans[i - 1].start)):
                 pair = sliced[i - 1][none, :, half]
                 found = dot(pair, pair, NT)
                 gram, off = two_sum(gram, found[:size, :size])
@@ -403,31 +410,26 @@
     mixed = mixed + close_product(mixed, change, NT)
     coupling_held[...] = mixed
     left = left_terms(jnp.concatenate([whole * scale, product(mixed, whole, NN)], axis=0))
-    stores = []
 
     def store(src, dst, place):
-        stores.append(pltpu.make_async_copy(src, dst, store_sem.at[place]))
-        stores[-1].start()
-
+        pltpu.make_async_copy(src, dst, store_sem.at[place]).start()
+
+    store(coupling_held, coupling, 2)
     for i in range(steps):
         span, at = slice(i * chunk, (i + 1) * chunk), pl.ds(i * chunk, chunk)
         one, two, three = (pieces[t * size : (t + 1) * size, span] for t in range(3))
-        right = jnp.concatenate([one, three, two, one, two, one], axis=0)
-        out = dot(left, right, NN)
+        out = dot(left, jnp.concatenate([one, three, two, one, two, one], axis=0), NN)
         basis_held[:, span] = out[:size]
-        store(basis_held.at[:, at], basis.at[:, at], 2 * i)
-        projected = out[size:]
-        updated_held[:, span] = trailing[:, span] - projected
-        store(updated_held.at[:, at], updated.at[:, at], 2 * i + 1)
-        if i == steps - 1:
-            row = lax.broadcasted_iota(jnp.int32, (size, size), 0)
-            lane = lax.broadcasted_iota(jnp.int32, (size, size), 1)
-            total = product(whole, gram[...], NN) + dot(whole.astype(jnp.bfloat16), lost.astype(jnp.bfloat16), NN)
-            upper_held[...] = jnp.where(row <= lane, total * (1.0 / scale), 0.0)
-            store(coupling_held, coupling, 2 * steps)
-            store(upper_held, upper, 2 * steps + 1)
-    for copy in stores:
-        copy.wait()
+        store(basis_held.at[:, at], basis.at[:, at], 0)
+        updated_held[:, span] = trailing[:, span] - out[size:]
+        store(updated_held.at[:, at], updated.at[:, at], 1)
+    row = lax.broadcasted_iota(jnp.int32, (size, size), 0)
+    lane = lax.broadcasted_iota(jnp.int32, (size, size), 1)
+    total = product(whole, gram[...], NN) + dot(whole.astype(jnp.bfloat16), lost.astype(jnp.bfloat16), NN)
+    upper_held[...] = jnp.where(row <= lane, total * (1.0 / scale), 0.0)
+    store(upper_held, upper, 3)
+    for place, (src, dst) in enumerate(((basis_held, basis), (updated_held, updated), (coupling_held, coupling), (upper_held, upper))):
+        pltpu.make_async_copy(src, dst, store_sem.at[place]).wait()
 
 
 def shards(sizes, panel, trailing):
@@ -460,10 +462,10 @@
         out_specs=[VMEM] * 7,
         scratch_shapes=[
             pltpu.VMEM((size, width), f32),
-            pltpu.SemaphoreType.DMA((width // chunk_of(width, 1024) + 1,)),
+            pltpu.SemaphoreType.DMA((len(spans_of(width)) + 1,)),
             *exchange_scratch(sizes, rows, size),
             *exchange_scratch(sizes, rows + less, size),
-            *[pltpu.VMEM((1, 2 * size, chunk_of(width, 1024)), jnp.bfloat16) for _ in range(width // chunk_of(width, 1024))],
+            *[pltpu.VMEM((1, 2 * size, span.stop - span.start), jnp.bfloat16) for span in spans_of(width)],
         ],
         compiler_params=params(0),
         name="reduce",
@@ -483,7 +485,7 @@
             pltpu.VMEM((trail, width), f32),
             pltpu.VMEM((size, size), f32),
             pltpu.VMEM((trail, size), f32),
-            pltpu.SemaphoreType.DMA((2 * (width // chunk_of(width, 512)) + 2,)),
+            pltpu.SemaphoreType.DMA((4,)),
         ],
         compiler_params=params(),
         name="final",

time: 23.1 us -> 23 us (level)
  no operation moved by 1% of the time
where the time goes in v9:
time: 23 us; the launch traced here: 22.8 us
  Pallas kernels  22.2 us (97%)
  between operations  0.64 us (3%)
    pallas_call x1, Pallas kernels, shards(): pl.pallas_call(functools.partial(reduce_kernel, sizes), out_shape=[square...  19.2 us
    pallas_call x1, Pallas kernels, shards(): pl.pallas_call(functools.partial(final_kernel, scale), out_shape=[jax.Sha...  3.01 us

profile of v9, /device:TPU:0, one launch (start us, length us, event | category | flops | bytes accessed | tf_op | source)
XLA Modules:
  0.0 22.8 jit_solution(17800834880319766283)
XLA Ops:
  0.6 19.2 %reduce.1 = (f32[128,128]{1,0:T(8,128)S(1)}, f32[8,24,128]{2,1,0:T(8,128)S(1)}, f32[128,128]{1,0:T(8,128)S(1)}, f32[128,128]{1,0:T(8,128)S(1)}, f32[128,128]{1,0...) custom-call(f32[128,4096]{1,0:T(8,128)} %panel.1, f32[64,4096]{1,0:T(8,128)} %trailing.1), custom_call_target="tpu_custom_call" | custom-call | tf_op jit(solution)/shard_map/reduce/pallas_call | solution.py:450
  19.8 3.0 %final.1 = (f32[128,4096]{1,0:T(8,128)}, f32[128,128]{1,0:T(8,128)}, f32[64,128]{1,0:T(8,128)}, f32[64,4096]{1,0:T(8,128)}) custom-call(f32[128,128]{1,0:T(8,128)S(1)} %get-tuple-element.15.gram, f32[8,24,128]{2,1,0:T(8,128)S(1)} %get-tuple-element.16.rest, f32[128,128]{1,0:T(8,128)S(1)} %get-tuple-element.17.off, f32[128,128]{1,0:T(8,128)S(1)} %get-tuple-element.18.turned, ...), custom_call_target="tpu_custom_call" | custom-call | tf_op jit(solution)/shard_map/final/pallas_call | solution.py:473
